TPU v7x, 768 devices: a whole 4x8x12 slice. The times are simulated.
768 devices in a mesh: gx: 24 (over z, core), gy: 8 (over x, y_lo), gz: 4 (over y_hi).
Axes of the slice: x: 4, y: 8 (y_hi: 4, y_lo: 2; y = y_hi * 2 + y_lo), z: 12, core: 2. Of those that a mesh axis runs over, the one named last changes fastest.
Arguments:
- positions: float32 [24, 8, 8, 192], P('gx', 'gy', 'gz'), may hold values from 0 to 1, as said below
- species: int32 [24, 8, 8, 64], P('gx', 'gy', 'gz'), may hold values from 0 to 4
- neighbors: int32 [24, 8, 8, 512], P('gx', 'gy', 'gz'), may hold values from 0 to 1727, as said below
- center_table: bfloat16 [5, 128], replicated, may hold values from -4 to 4
- neighbor_table: bfloat16 [5, 128], replicated, may hold values from -4 to 4
- radial_weight: bfloat16 [8, 128], replicated, may hold values from -2 to 2
- mix_weight: bfloat16 [128, 128], replicated, may hold values from -0.5 to 0.5
- env_weight: bfloat16 [128, 128], replicated, may hold values from -0.5 to 0.5
- update_weight: bfloat16 [384, 128], replicated, may hold values from -0.3125 to 0.3125
- second_weight: bfloat16 [128, 128], replicated, may hold values from -0.5 to 0.5
- readout: float32 [128], replicated, may hold values from -0.5 to 0.5
Outputs:
- atom_energy: float32 [24, 8, 8, 64], P('gx', 'gy', 'gz')
- forces: float32 [24, 8, 8, 192], P('gx', 'gy', 'gz')
Inputs may be any that keep to these rules, and one draw needn't show every extreme that they name: `positions`: every coordinate lies inside its block; atoms of a block sit on a jittered sublattice, so any two atoms are at least 0.4 / cube root of 64 apart. `neighbors`: each atom lists 8 different atoms of the 27 blocks around and including its own, never itself; a code is offset index times 64 plus slot.
All inputs are finite; a program needn't handle non-finite values.
Results may differ from a plain program's by a relative error of at most 0.011.
Values may be sent and summed in bfloat16 or wider, within the bound.
A program may use at most 32 MiB of HBM per device.

v0:
```python
import math

import jax
import jax.numpy as jnp
from jax import lax
from jax.sharding import PartitionSpec as P

NEIGH = 8


CUTOFF = 4.0
SHARPNESS = 2.0
HIGH = lax.Precision.HIGHEST


def padded_2(cells, sides, width):
    for axis, dim in sides:
        count = lax.axis_size(axis)
        head = lax.slice_in_dim(cells, 0, width, axis=dim)
        tail = lax.slice_in_dim(cells, cells.shape[dim] - width, cells.shape[dim], axis=dim)
        cells = jnp.concatenate(
            [
                lax.ppermute(tail, axis, [(i, (i + 1) % count) for i in range(count)]),
                cells,
                lax.ppermute(head, axis, [((i + 1) % count, i) for i in range(count)]),
            ],
            axis=dim,
        )
    return cells


def harmonics(displacement):
    distance = jnp.sqrt(jnp.sum(displacement * displacement, axis=0))
    unit_vec = displacement / distance
    unit_x, unit_y, unit_z = (unit_vec[0], unit_vec[1], unit_vec[2])
    root_three = math.sqrt(3.0)
    angular = jnp.stack(
        [
            jnp.ones_like(unit_x),
            unit_x,
            unit_y,
            unit_z,
            root_three * unit_x * unit_y,
            root_three * unit_y * unit_z,
            0.5 * (3.0 * unit_z * unit_z - 1.0),
            root_three * unit_x * unit_z,
            0.5 * root_three * (unit_x * unit_x - unit_y * unit_y),
        ],
        axis=0,
    )
    return (distance, angular)


def layer_one(displacement, onehot_center, onehot_other, params):
    radial_weight, center_table, neighbor_table, mix_weight, env_weight, update_weight = params
    distance, angular = harmonics(displacement)
    nbasis = radial_weight.shape[0]
    centers = CUTOFF * (jnp.arange(nbasis, dtype=jnp.float32) + 0.5) / nbasis
    cut_ratio = distance / CUTOFF
    envelope = (1.0 - cut_ratio * cut_ratio) ** 2
    radial_basis = (
        jnp.exp(-SHARPNESS * (distance[:, None] - centers[None, :]) ** 2) * envelope[:, None]
    )
    before = jnp.dot(
        radial_basis.astype(jnp.bfloat16), radial_weight, preferred_element_type=jnp.float32
    )
    before = before + jnp.dot(onehot_center, center_table, preferred_element_type=jnp.float32)
    before = before + jnp.dot(onehot_other, neighbor_table, preferred_element_type=jnp.float32)
    activated = jax.nn.silu(before).astype(jnp.bfloat16)
    latent = jax.nn.silu(jnp.dot(activated, mix_weight, preferred_element_type=jnp.float32))
    env_terms = jnp.dot(latent.astype(jnp.bfloat16), env_weight, preferred_element_type=jnp.float32)
    channels = latent.shape[1]
    center_count = latent.shape[0] // NEIGH
    env_terms = env_terms.reshape(center_count, NEIGH, channels)
    harmonic_grid = angular.reshape(9, center_count, NEIGH)
    environment = jnp.einsum("akc,mak->amc", env_terms, harmonic_grid, precision=HIGH) / NEIGH
    pieces = []
    for start_m, stop_m in ((0, 1), (1, 4), (4, 9)):
        pieces.append(
            jnp.einsum(
                "amc,mak->akc",
                environment[:, start_m:stop_m],
                harmonic_grid[start_m:stop_m],
                precision=HIGH,
            )
        )
    invariants = jnp.concatenate(pieces, axis=2).reshape(center_count * NEIGH, 3 * channels)
    invariants = invariants.astype(jnp.bfloat16)
    update = jnp.dot(invariants, update_weight, preferred_element_type=jnp.float32)
    edge_latent = jax.nn.silu(latent + update)
    atom_latent = jnp.mean(edge_latent.reshape(center_count, NEIGH, channels), axis=1)
    return (atom_latent, edge_latent)


def layer_two(edge_latent, other_latent, second_weight, readout):
    product = (edge_latent * other_latent).astype(jnp.bfloat16)
    hidden = jax.nn.silu(jnp.dot(product, second_weight, preferred_element_type=jnp.float32))
    edge_energy = jnp.dot(hidden, readout, precision=HIGH)
    return jnp.sum(edge_energy.reshape(-1, NEIGH), axis=1)


def edge_model(rel_center, rel_other, offsets, onehot_center, onehot_other, params):
    displacement = (offsets + (rel_other - rel_center[:, :, None])).reshape(3, -1)
    return layer_one(displacement, onehot_center, onehot_other, params)


def one_hot(labels, count):
    return (labels[:, None] == jnp.arange(count, dtype=jnp.int32)[None, :]).astype(jnp.bfloat16)


def fold_rim(extended, dimension, interior):
    middle = lax.slice_in_dim(extended, 2, 2 + interior, axis=dimension)
    leading = lax.slice_in_dim(extended, 0, 1, axis=dimension)
    trailing = lax.slice_in_dim(extended, interior + 3, interior + 4, axis=dimension)
    front_pad = [(0, 0)] * extended.ndim
    front_pad[dimension] = (0, interior - 1)
    back_pad = [(0, 0)] * extended.ndim
    back_pad[dimension] = (interior - 1, 0)
    return middle + jnp.pad(leading, front_pad) + jnp.pad(trailing, back_pad)


def on_device(
    positions,
    species,
    neighbors,
    center_table,
    neighbor_table,
    radial_weight,
    mix_weight,
    env_weight,
    update_weight,
    second_weight,
    readout,
):
    params = (radial_weight, center_table, neighbor_table, mix_weight, env_weight, update_weight)
    cells_x, cells_y, cells_z, triple = positions.shape
    slot_count = triple // 3
    channels = mix_weight.shape[1]
    outer_x, outer_y, outer_z = (cells_x + 2, cells_y + 2, cells_z + 2)
    atom_count = cells_x * cells_y * cells_z * slot_count
    padded_count = outer_x * outer_y * outer_z * slot_count
    packed = jnp.concatenate([positions, species.astype(jnp.float32)], axis=3)
    padded = padded_2(packed, (("gx", 0), ("gy", 1), ("gz", 2)), 1)
    ghost_pos = padded[..., :triple].reshape(outer_x, outer_y, outer_z, 3, slot_count)
    ghost_pos = ghost_pos.transpose(3, 0, 1, 2, 4).reshape(3, padded_count)
    ghost_species = padded[..., triple:].reshape(padded_count).astype(jnp.int32)
    index_x = jnp.arange(cells_x, dtype=jnp.int32).reshape(cells_x, 1, 1, 1, 1)
    index_y = jnp.arange(cells_y, dtype=jnp.int32).reshape(1, cells_y, 1, 1, 1)
    index_z = jnp.arange(cells_z, dtype=jnp.int32).reshape(1, 1, cells_z, 1, 1)
    codes = neighbors.reshape(cells_x, cells_y, cells_z, slot_count, NEIGH)
    offset_code = codes // slot_count
    slot_other = codes % slot_count
    step_x = offset_code // 9 - 1
    step_y = offset_code // 3 % 3 - 1
    step_z = offset_code % 3 - 1
    cell_other = ((index_x + 1 + step_x) * outer_y + (index_y + 1 + step_y)) * outer_z + (
        index_z + 1 + step_z
    )
    other_index = (cell_other * slot_count + slot_other).reshape(atom_count, NEIGH)
    other_flat = other_index.reshape(-1)
    slot_own = jnp.arange(slot_count, dtype=jnp.int32).reshape(1, 1, 1, slot_count)
    cell_own = (
        ((index_x[..., 0] + 1) * outer_y + index_y[..., 0] + 1) * outer_z + index_z[..., 0] + 1
    )
    own_index = (cell_own * slot_count + slot_own).reshape(atom_count)
    offsets = jnp.stack([step_x, step_y, step_z]).astype(jnp.float32).reshape(3, atom_count, NEIGH)
    spec_count = center_table.shape[0]
    center_species = jnp.broadcast_to(
        species.reshape(atom_count)[:, None], (atom_count, NEIGH)
    ).reshape(-1)
    onehot_center = one_hot(center_species, spec_count)
    onehot_other = one_hot(ghost_species[other_flat], spec_count)
    rel_center = ghost_pos[:, own_index]
    rel_other = ghost_pos[:, other_index]

    def first(center_pos, other_pos):
        return edge_model(center_pos, other_pos, offsets, onehot_center, onehot_other, params)

    outputs, back_one = jax.vjp(first, rel_center, rel_other)
    coarse_table = (
        outputs[0].astype(jnp.bfloat16).reshape(cells_x, cells_y, cells_z, slot_count * channels)
    )
    spread_latent = padded_2(coarse_table, (("gx", 0), ("gy", 1), ("gz", 2)), 1)
    latent_table = spread_latent.reshape(padded_count, channels)
    other_latent = latent_table[other_flat].astype(jnp.float32)

    def second(edge_latent, neighbor_latent):
        return layer_two(edge_latent, neighbor_latent, second_weight, readout)

    energy, back_two = jax.vjp(second, outputs[1], other_latent)
    grad_edge, grad_other = back_two(jnp.ones_like(energy))
    latent_spread = jnp.zeros((padded_count, channels), jnp.float32).at[other_flat].add(grad_other)
    latent_spread = latent_spread.reshape(outer_x, outer_y, outer_z, slot_count * channels)
    returned = padded_2(latent_spread, (("gx", 0), ("gy", 1), ("gz", 2)), 1)
    owned_grad = fold_rim(fold_rim(fold_rim(returned, 0, cells_x), 1, cells_y), 2, cells_z)
    grad_center, grad_other_pos = back_one((owned_grad.reshape(atom_count, channels), grad_edge))
    motion = jnp.zeros((3, padded_count), jnp.float32).at[:, own_index].add(grad_center)
    motion = motion.at[:, other_flat].add(grad_other_pos.reshape(3, -1))
    motion = motion.reshape(3, outer_x, outer_y, outer_z, slot_count).transpose(1, 2, 3, 0, 4)
    motion = motion.reshape(outer_x, outer_y, outer_z, triple)
    returned_motion = padded_2(motion, (("gx", 0), ("gy", 1), ("gz", 2)), 1)
    forces = -fold_rim(fold_rim(fold_rim(returned_motion, 0, cells_x), 1, cells_y), 2, cells_z)
    return (energy.reshape(cells_x, cells_y, cells_z, slot_count), forces)


def solution(mesh):
    placed = (
        P("gx", "gy", "gz", None),
        P("gx", "gy", "gz", None),
        P("gx", "gy", "gz", None),
        P(),
        P(),
        P(),
        P(),
        P(),
        P(),
        P(),
        P(),
    )
    return jax.shard_map(
        on_device,
        mesh=mesh,
        in_specs=placed,
        out_specs=(P("gx", "gy", "gz", None), P("gx", "gy", "gz", None)),
        check_vma=False,
    )
```

profile of v0, /device:TPU:28, one launch (start us, length us, event | category | flops | bytes accessed | tf_op | source)
XLA Modules:
  0.0 257.8 jit_solution(15477085415574577539)
XLA Ops:
  2.1 12.1 %collective-permute-start.1 = (f32[1,1,2,256]{3,2,1,0:T(2,128)S(1)}, f32[1,1,2,256]{3,2,1,0:T(2,128)S(1)}, u32[]{:S(2)}, u32[]{:S(2)}) collective-permute-start(f32[1,1,2,256]{3,2,1,0:T(2,128)S(1)} %pad_maximum_fusion.35), channel_id=1, source_target_pairs={{32,0},{64,32},{96,64},{128,96},{160,128},{192,160},{224,192},{256... | collective-permute-start | bytes 6152 | tf_op jit(solution)/shard_map/ppermute | solution.py:25
  21.6 4.4 %collective-permute-start.2 = (f32[3,1,2,256]{3,2,1,0:T(2,128)S(1)}, f32[3,1,2,256]{3,2,1,0:T(2,128)S(1)}, u32[]{:S(2)}, u32[]{:S(2)}) collective-permute-start(f32[3,1,2,256]{3,2,1,0:T(2,128)S(1)} %pad_maximum_fusion.34), channel_id=1, source_target_pairs={{0,4},{4,8},{8,12},{12,16},{16,20},{20,24},{24,28},{28,0},{1,5},{5... | collective-permute-start | bytes 18440 | tf_op jit(solution)/shard_map/ppermute | solution.py:23
  28.1 5.5 %collective-permute-start.4 = (f32[3,3,1,256]{3,2,1,0:T(1,128)S(1)}, f32[3,3,1,256]{3,2,1,0:T(1,128)S(1)}, u32[]{:S(2)}, u32[]{:S(2)}) collective-permute-start(f32[3,3,1,256]{3,2,1,0:T(1,128)S(1)} %get-tuple-element.48), channel_id=1, source_target_pairs={{0,1},{1,2},{2,3},{3,0},{4,5},{5,6},{6,7},{7,4},{8,9},{9,10},{10,1... | collective-permute-start | bytes 27656 | tf_op jit(solution)/shard_map/ppermute | solution.py:23
  36.7 4.6 %collective-permute-done.5 = f32[3,3,1,256]{3,2,1,0:T(1,128)S(1)} collective-permute-done((f32[3,3,1,256]{3,2,1,0:T(1,128)S(1)}, f32[3,3,1,256]{3,2,1,0:T(1,128)S(1)}, u32[]{:S(2)}, u32[]{:S(2)}) %collective-permute-start.5) | collective-permute-done | bytes 9248 | tf_op jit(solution)/shard_map/ppermute | solution.py:25
  42.7 2.8 %gather_fusion = f32[1024,3]{1,0:T(8,128)S(1)} fusion(f32[3,2304]{0,1:T(8,128)S(1)} %bitcast.99, s32[1024]{0:T(1024)S(1)} %broadcast_clamp_fusion.1), kind=kCustom, calls=%fused_computation | custom fusion | bytes 28672 | tf_op jit(solution)/shard_map/gather | solution.py:174
  49.8 6.2 %gather_fusion.2 = s32[1024]{0:T(1024)S(1)} fusion(s32[2304]{0:T(1024)S(1)} %convert_element_type.95, s32[1024]{0:T(1024)S(1)} %get-tuple-element.65), kind=kCustom, calls=%fused_computation.2 | custom fusion | bytes 12288 | tf_op jit(solution)/shard_map/gather | solution.py:172
  63.1 2.9 %collective-permute-start.7 = (bf16[1,1,2,8192]{3,2,1,0:T(2,128)(2,1)S(1)}, bf16[1,1,2,8192]{3,2,1,0:T(2,128)(2,1)S(1)}, u32[]{:S(2)}, u32[]{:S(2)}) collective-permute-start(bf16[1,1,2,8192]{3,2,1,0:T(2,128)(2,1)S(1)} %convert_element_type.101), channel_id=1, source_target_pairs={{32,0},{64,32},{96,64},{128,96},{160,128},{192,160},{224,192},{256... | collective-permute-start | bytes 98312 | tf_op jit(solution)/shard_map/ppermute | solution.py:25
  67.7 3.5 %collective-permute-start.9 = (bf16[3,1,2,8192]{3,2,1,0:T(2,128)(2,1)S(1)}, bf16[3,1,2,8192]{3,2,1,0:T(2,128)(2,1)S(1)}, u32[]{:S(2)}, u32[]{:S(2)}) collective-permute-start(bf16[3,1,2,8192]{3,2,1,0:T(2,128)(2,1)S(1)} %constant_dynamic-update-slice_fusion.7), channel_id=1, source_target_pairs={{4,0},{8,4},{12,8},{16,12},{20,16},{24,20},{28,24},{0,28},{5,1},{9... | collective-permute-start | bytes 294920 | tf_op jit(solution)/shard_map/ppermute | solution.py:25
  71.2 3.3 %collective-permute-start.8 = (bf16[3,1,2,8192]{3,2,1,0:T(2,128)(2,1)S(1)}, bf16[3,1,2,8192]{3,2,1,0:T(2,128)(2,1)S(1)}, u32[]{:S(2)}, u32[]{:S(2)}) collective-permute-start(bf16[3,1,2,8192]{3,2,1,0:T(2,128)(2,1)S(1)} %constant_dynamic-update-slice_fusion.7), channel_id=1, source_target_pairs={{0,4},{4,8},{8,12},{12,16},{16,20},{20,24},{24,28},{28,0},{1,5},{5... | collective-permute-start | bytes 294920 | tf_op jit(solution)/shard_map/ppermute | solution.py:23
  75.2 2.5 collective-permute-done.8
  80.7 5.0 %collective-permute-start.11 = (bf16[3,3,1,8192]{3,2,1,0:T(2,128)(2,1)S(1)}, bf16[3,3,1,8192]{3,2,1,0:T(2,128)(2,1)S(1)}, u32[]{:S(2)}, u32[]{:S(2)}) collective-permute-start(bf16[3,3,1,8192]{3,2,1,0:T(2,128)(2,1)S(1)} %get-tuple-element.35), channel_id=1, source_target_pairs={{1,0},{2,1},{3,2},{0,3},{5,4},{6,5},{7,6},{4,7},{9,8},{10,9},{11,1... | collective-permute-start | bytes 442376 | tf_op jit(solution)/shard_map/ppermute | solution.py:25
  85.7 6.6 %collective-permute-done.10 = bf16[3,3,1,8192]{3,2,1,0:T(2,128)(2,1)S(1)} collective-permute-done((bf16[3,3,1,8192]{3,2,1,0:T(2,128)(2,1)S(1)}, bf16[3,3,1,8192]{3,2,1,0:T(2,128)(2,1)S(1)}, u32[]{:S(2)}, u32[]{:S(2)}) %collective-permute-start.10) | collective-permute-done | bytes 147488 | tf_op jit(solution)/shard_map/ppermute | solution.py:23
  96.3 3.2 %gather_fusion.3 = bf16[1024,128]{1,0:T(8,128)(2,1)S(1)} fusion(bf16[2304,128]{1,0:T(8,128)(2,1)S(1)} %reshape.1254, s32[1024]{0:T(1024)S(1)} %get-tuple-element.65), kind=kCustom, calls=%fused_computation.3 | custom fusion | bytes 528384 | tf_op jit(solution)/shard_map/gather | solution.py:185
  102.3 6.6 %scatter_custom_fusion = f32[2304,128]{1,0:T(8,128)S(1)} fusion(s32[1024]{0:T(1024)} %bitcast.110, f32[]{:T(128)} %constant.112.clone.1, f32[1024,128]{1,0:T(8,128)S(1)} %fusion.5, f32[1024,128]{1,0:T(8,128)S(1)} %copy-done.10), kind=kCustom, calls=%fused_computation.47 | custom fusion | flops 786432 | bytes 2228736 | tf_op jit(solution)/shard_map/scatter-add | solution.py:192
  112.3 5.6 %collective-permute-start.13 = (f32[1,3,4,8192]{3,2,1,0:T(4,128)S(1)}, f32[1,3,4,8192]{3,2,1,0:T(4,128)S(1)}, u32[]{:S(2)}, u32[]{:S(2)}) collective-permute-start(f32[1,3,4,8192]{3,2,1,0:T(4,128)S(1)} %slice.179), channel_id=1, source_target_pairs={{32,0},{64,32},{96,64},{128,96},{160,128},{192,160},{224,192},{256... | collective-permute-start | bytes 1179656 | tf_op jit(solution)/shard_map/ppermute | solution.py:25
  117.8 4.1 %collective-permute-done.12 = f32[1,3,4,8192]{3,2,1,0:T(4,128)} collective-permute-done((f32[1,3,4,8192]{3,2,1,0:T(4,128)}, f32[1,3,4,8192]{3,2,1,0:T(4,128)}, u32[]{:S(2)}, u32[]{:S(2)}) %collective-permute-start.12) | collective-permute-done | bytes 393248 | tf_op jit(solution)/shard_map/ppermute | solution.py:23
  123.3 4.3 %collective-permute-start.14 = (f32[5,1,4,8192]{3,2,1,0:T(4,128)S(1)}, f32[5,1,4,8192]{3,2,1,0:T(4,128)S(1)}, u32[]{:S(2)}, u32[]{:S(2)}) collective-permute-start(f32[5,1,4,8192]{3,2,1,0:T(4,128)S(1)} %get-tuple-element.30), channel_id=1, source_target_pairs={{0,4},{4,8},{8,12},{12,16},{16,20},{20,24},{24,28},{28,0},{1,5},{5... | collective-permute-start | bytes 1966088 | tf_op jit(solution)/shard_map/ppermute | solution.py:23
  129.6 11.4 %collective-permute-done.14 = f32[5,1,4,8192]{3,2,1,0:T(4,128)S(1)} collective-permute-done((f32[5,1,4,8192]{3,2,1,0:T(4,128)S(1)}, f32[5,1,4,8192]{3,2,1,0:T(4,128)S(1)}, u32[]{:S(2)}, u32[]{:S(2)}) %collective-permute-start.14) | collective-permute-done | bytes 655392 | tf_op jit(solution)/shard_map/ppermute | solution.py:23
  141.0 7.7 %collective-permute-done.15 = f32[5,1,4,8192]{3,2,1,0:T(4,128)S(1)} collective-permute-done((f32[5,1,4,8192]{3,2,1,0:T(4,128)S(1)}, f32[5,1,4,8192]{3,2,1,0:T(4,128)S(1)}, u32[]{:S(2)}, u32[]{:S(2)}) %collective-permute-start.15) | collective-permute-done | bytes 655392 | tf_op jit(solution)/shard_map/ppermute | solution.py:25
  150.5 4.4 %collective-permute-start.16 = (f32[5,5,1,8192]{3,2,1,0:T(1,128)S(1)}, f32[5,5,1,8192]{3,2,1,0:T(1,128)S(1)}, u32[]{:S(2)}, u32[]{:S(2)}) collective-permute-start(f32[5,5,1,8192]{3,2,1,0:T(1,128)S(1)} %get-tuple-element.28), channel_id=1, source_target_pairs={{0,1},{1,2},{2,3},{3,0},{4,5},{5,6},{6,7},{7,4},{8,9},{9,10},{10,1... | collective-permute-start | bytes 2457608 | tf_op jit(solution)/shard_map/ppermute | solution.py:23
  155.0 2.7 %collective-permute-start.17 = (f32[5,5,1,8192]{3,2,1,0:T(1,128)S(1)}, f32[5,5,1,8192]{3,2,1,0:T(1,128)S(1)}, u32[]{:S(2)}, u32[]{:S(2)}) collective-permute-start(f32[5,5,1,8192]{3,2,1,0:T(1,128)S(1)} %get-tuple-element.29), channel_id=1, source_target_pairs={{1,0},{2,1},{3,2},{0,3},{5,4},{6,5},{7,6},{4,7},{9,8},{10,9},{11,1... | collective-permute-start | bytes 2457608 | tf_op jit(solution)/shard_map/ppermute | solution.py:25
  157.7 25.4 %collective-permute-done.16 = f32[5,5,1,8192]{3,2,1,0:T(1,128)S(1)} collective-permute-done((f32[5,5,1,8192]{3,2,1,0:T(1,128)S(1)}, f32[5,5,1,8192]{3,2,1,0:T(1,128)S(1)}, u32[]{:S(2)}, u32[]{:S(2)}) %collective-permute-start.16) | collective-permute-done | bytes 819232 | tf_op jit(solution)/shard_map/ppermute | solution.py:23
  183.1 4.5 %collective-permute-done.17 = f32[5,5,1,8192]{3,2,1,0:T(1,128)S(1)} collective-permute-done((f32[5,5,1,8192]{3,2,1,0:T(1,128)S(1)}, f32[5,5,1,8192]{3,2,1,0:T(1,128)S(1)}, u32[]{:S(2)}, u32[]{:S(2)}) %collective-permute-start.17) | collective-permute-done | bytes 819232 | tf_op jit(solution)/shard_map/ppermute | solution.py:25
  196.0 2.4 fusion.111
  198.4 2.8 %fusion.1 = f32[9,128,8]{0,2,1:T(8,128)S(1)} fusion(f32[128,8,128]{2,1,0:T(8,128)S(1)} %copy-done.8, f32[128,1,128]{2,1,0:T(1,128)} %copy-done.21, f32[128,3,128]{2,1,0:T(4,128)S(1)} %fusion.68, f32[128,5,128]{2,1,0:T(8,128)S(1)} %fusion.30, f32[1,128,8]{0,2,1:T(8,128)S(1)} %convolution_bitcast_fusion.2, f32[3,128,8]{0,2,1:T(8,128)S(1)} %convolution_bitcast_fusion.3, ...), kind=kOutput, calls=%fused_computation.14 | convolution fusion | flops 14625792 | bytes 1187840 | tf_op jit(solution)/shard_map/transpose(jvp(akc,mak->amc))/dot_general | solution.py:76
  206.9 6.5 %scatter_fusion = f32[3,2304]{0,1:T(8,128)S(1)} fusion(f32[3,2304]{0,1:T(8,128)S(1)} %scatter_custom_fusion.1, s32[1024]{0:T(1024)S(1)} %bitcast.111, f32[1024,3]{1,0:T(8,128)S(1)} %copy.213), kind=kCustom, calls=%fused_computation.6 | custom fusion | flops 3072 | bytes 40960 | tf_op jit(solution)/shard_map/scatter-add | solution.py:198
  214.1 3.0 %collective-permute-start.19 = (f32[1,3,4,192]{3,2,1,0:T(4,128)S(1)}, f32[1,3,4,192]{3,2,1,0:T(4,128)S(1)}, u32[]{:S(2)}, u32[]{:S(2)}) collective-permute-start(f32[1,3,4,192]{3,2,1,0:T(4,128)S(1)} %slice.197), channel_id=1, source_target_pairs={{32,0},{64,32},{96,64},{128,96},{160,128},{192,160},{224,192},{256... | collective-permute-start | bytes 27656 | tf_op jit(solution)/shard_map/ppermute | solution.py:25
  220.5 18.6 %collective-permute-start.20 = (f32[5,1,4,192]{3,2,1,0:T(4,128)S(1)}, f32[5,1,4,192]{3,2,1,0:T(4,128)S(1)}, u32[]{:S(2)}, u32[]{:S(2)}) collective-permute-start(f32[5,1,4,192]{3,2,1,0:T(4,128)S(1)} %get-tuple-element.43), channel_id=1, source_target_pairs={{0,4},{4,8},{8,12},{12,16},{16,20},{20,24},{24,28},{28,0},{1,5},{5... | collective-permute-start | bytes 46088 | tf_op jit(solution)/shard_map/ppermute | solution.py:23
  241.1 4.6 %collective-permute-done.21 = f32[5,1,4,192]{3,2,1,0:T(4,128)S(1)} collective-permute-done((f32[5,1,4,192]{3,2,1,0:T(4,128)S(1)}, f32[5,1,4,192]{3,2,1,0:T(4,128)S(1)}, u32[]{:S(2)}, u32[]{:S(2)}) %collective-permute-start.21) | collective-permute-done | bytes 15392 | tf_op jit(solution)/shard_map/ppermute | solution.py:25
  245.7 3.5 %collective-permute-start.22 = (f32[5,5,1,192]{3,2,1,0:T(1,128)S(1)}, f32[5,5,1,192]{3,2,1,0:T(1,128)S(1)}, u32[]{:S(2)}, u32[]{:S(2)}) collective-permute-start(f32[5,5,1,192]{3,2,1,0:T(1,128)S(1)} %get-tuple-element.36), channel_id=1, source_target_pairs={{0,1},{1,2},{2,3},{3,0},{4,5},{5,6},{6,7},{7,4},{8,9},{9,10},{10,1... | collective-permute-start | bytes 57608 | tf_op jit(solution)/shard_map/ppermute | solution.py:23
  249.2 3.3 %collective-permute-start.23 = (f32[5,5,1,192]{3,2,1,0:T(1,128)S(1)}, f32[5,5,1,192]{3,2,1,0:T(1,128)S(1)}, u32[]{:S(2)}, u32[]{:S(2)}) collective-permute-start(f32[5,5,1,192]{3,2,1,0:T(1,128)S(1)} %get-tuple-element.37), channel_id=1, source_target_pairs={{1,0},{2,1},{3,2},{0,3},{5,4},{6,5},{7,6},{4,7},{9,8},{10,9},{11,1... | collective-permute-start | bytes 57608 | tf_op jit(solution)/shard_map/ppermute | solution.py:25
  254.1 3.0 %collective-permute-done.23 = f32[5,5,1,192]{3,2,1,0:T(1,128)S(1)} collective-permute-done((f32[5,5,1,192]{3,2,1,0:T(1,128)S(1)}, f32[5,5,1,192]{3,2,1,0:T(1,128)S(1)}, u32[]{:S(2)}, u32[]{:S(2)}) %collective-permute-start.23) | collective-permute-done | bytes 19232 | tf_op jit(solution)/shard_map/ppermute | solution.py:25
  (273 shorter events, 68.9 us)
Async XLA Ops:
  0.6 61.8 %copy-start = (bf16[384,128]{1,0:T(8,128)(2,1)S(1)}, bf16[384,128]{1,0:T(8,128)(2,1)}, u32[]{:S(2)}) copy-start(bf16[384,128]{1,0:T(8,128)(2,1)} %param.19) | copy-start | bytes 294916
  0.6 40.6 %copy-start.26 = (f32[1,1,2,192]{3,2,1,0:T(2,128)S(1)}, f32[1,1,2,192]{3,2,1,0:T(2,128)}, u32[]{:S(2)}) copy-start(f32[1,1,2,192]{3,2,1,0:T(2,128)} %param.11) | copy-start | bytes 4612
  2.1 16.3 %collective-permute-start.1 = (f32[1,1,2,256]{3,2,1,0:T(2,128)S(1)}, f32[1,1,2,256]{3,2,1,0:T(2,128)S(1)}, u32[]{:S(2)}, u32[]{:S(2)}) collective-permute-start(f32[1,1,2,256]{3,2,1,0:T(2,128)S(1)} %pad_maximum_fusion.35), channel_id=1, source_target_pairs={{32,0},{64,32},{96,64},{128,96},{160,128},{192,160},{224,192},{256... | collective-permute-start | bytes 6152 | tf_op jit(solution)/shard_map/ppermute | solution.py:25
  14.2 4.2 %collective-permute-start = (f32[1,1,2,256]{3,2,1,0:T(2,128)S(1)}, f32[1,1,2,256]{3,2,1,0:T(2,128)S(1)}, u32[]{:S(2)}, u32[]{:S(2)}) collective-permute-start(f32[1,1,2,256]{3,2,1,0:T(2,128)S(1)} %pad_maximum_fusion.35), channel_id=1, source_target_pairs={{0,32},{32,64},{64,96},{96,128},{128,160},{160,192},{192,224},{224... | collective-permute-start | bytes 6152 | tf_op jit(solution)/shard_map/ppermute | solution.py:23
  19.2 6.8 %collective-permute-start.3 = (f32[3,1,2,256]{3,2,1,0:T(2,128)S(1)}, f32[3,1,2,256]{3,2,1,0:T(2,128)S(1)}, u32[]{:S(2)}, u32[]{:S(2)}) collective-permute-start(f32[3,1,2,256]{3,2,1,0:T(2,128)S(1)} %pad_maximum_fusion.34), channel_id=1, source_target_pairs={{4,0},{8,4},{12,8},{16,12},{20,16},{24,20},{28,24},{0,28},{5,1},{9... | collective-permute-start | bytes 18440 | tf_op jit(solution)/shard_map/ppermute | solution.py:25
  21.6 5.7 %collective-permute-start.2 = (f32[3,1,2,256]{3,2,1,0:T(2,128)S(1)}, f32[3,1,2,256]{3,2,1,0:T(2,128)S(1)}, u32[]{:S(2)}, u32[]{:S(2)}) collective-permute-start(f32[3,1,2,256]{3,2,1,0:T(2,128)S(1)} %pad_maximum_fusion.34), channel_id=1, source_target_pairs={{0,4},{4,8},{8,12},{12,16},{16,20},{20,24},{24,28},{28,0},{1,5},{5... | collective-permute-start | bytes 18440 | tf_op jit(solution)/shard_map/ppermute | solution.py:23
  28.1 8.6 %collective-permute-start.4 = (f32[3,3,1,256]{3,2,1,0:T(1,128)S(1)}, f32[3,3,1,256]{3,2,1,0:T(1,128)S(1)}, u32[]{:S(2)}, u32[]{:S(2)}) collective-permute-start(f32[3,3,1,256]{3,2,1,0:T(1,128)S(1)} %get-tuple-element.48), channel_id=1, source_target_pairs={{0,1},{1,2},{2,3},{3,0},{4,5},{5,6},{6,7},{7,4},{8,9},{9,10},{10,1... | collective-permute-start | bytes 27656 | tf_op jit(solution)/shard_map/ppermute | solution.py:23
  33.6 7.7 %collective-permute-start.5 = (f32[3,3,1,256]{3,2,1,0:T(1,128)S(1)}, f32[3,3,1,256]{3,2,1,0:T(1,128)S(1)}, u32[]{:S(2)}, u32[]{:S(2)}) collective-permute-start(f32[3,3,1,256]{3,2,1,0:T(1,128)S(1)} %get-tuple-element.49), channel_id=1, source_target_pairs={{1,0},{2,1},{3,2},{0,3},{5,4},{6,5},{7,6},{4,7},{9,8},{10,9},{11,1... | collective-permute-start | bytes 27656 | tf_op jit(solution)/shard_map/ppermute | solution.py:25
  63.0 36.5 %copy-start.9 = (f32[1024,128]{1,0:T(8,128)}, f32[1024,128]{1,0:T(8,128)S(1)}, u32[]{:S(2)}) copy-start(f32[1024,128]{1,0:T(8,128)S(1)} %get-tuple-element.63) | copy-start | bytes 1572868
  63.1 4.6 %collective-permute-start.6 = (bf16[1,1,2,8192]{3,2,1,0:T(2,128)(2,1)S(1)}, bf16[1,1,2,8192]{3,2,1,0:T(2,128)(2,1)S(1)}, u32[]{:S(2)}, u32[]{:S(2)}) collective-permute-start(bf16[1,1,2,8192]{3,2,1,0:T(2,128)(2,1)S(1)} %convert_element_type.101), channel_id=1, source_target_pairs={{0,32},{32,64},{64,96},{96,128},{128,160},{160,192},{192,224},{224... | collective-permute-start | bytes 98312 | tf_op jit(solution)/shard_map/ppermute | solution.py:23
  63.1 4.6 %collective-permute-start.7 = (bf16[1,1,2,8192]{3,2,1,0:T(2,128)(2,1)S(1)}, bf16[1,1,2,8192]{3,2,1,0:T(2,128)(2,1)S(1)}, u32[]{:S(2)}, u32[]{:S(2)}) collective-permute-start(bf16[1,1,2,8192]{3,2,1,0:T(2,128)(2,1)S(1)} %convert_element_type.101), channel_id=1, source_target_pairs={{32,0},{64,32},{96,64},{128,96},{160,128},{192,160},{224,192},{256... | collective-permute-start | bytes 98312 | tf_op jit(solution)/shard_map/ppermute | solution.py:25
  67.7 7.5 %collective-permute-start.9 = (bf16[3,1,2,8192]{3,2,1,0:T(2,128)(2,1)S(1)}, bf16[3,1,2,8192]{3,2,1,0:T(2,128)(2,1)S(1)}, u32[]{:S(2)}, u32[]{:S(2)}) collective-permute-start(bf16[3,1,2,8192]{3,2,1,0:T(2,128)(2,1)S(1)} %constant_dynamic-update-slice_fusion.7), channel_id=1, source_target_pairs={{4,0},{8,4},{12,8},{16,12},{20,16},{24,20},{28,24},{0,28},{5,1},{9... | collective-permute-start | bytes 294920 | tf_op jit(solution)/shard_map/ppermute | solution.py:25
  71.2 6.5 %collective-permute-start.8 = (bf16[3,1,2,8192]{3,2,1,0:T(2,128)(2,1)S(1)}, bf16[3,1,2,8192]{3,2,1,0:T(2,128)(2,1)S(1)}, u32[]{:S(2)}, u32[]{:S(2)}) collective-permute-start(bf16[3,1,2,8192]{3,2,1,0:T(2,128)(2,1)S(1)} %constant_dynamic-update-slice_fusion.7), channel_id=1, source_target_pairs={{0,4},{4,8},{8,12},{12,16},{16,20},{20,24},{24,28},{28,0},{1,5},{5... | collective-permute-start | bytes 294920 | tf_op jit(solution)/shard_map/ppermute | solution.py:23
  78.8 13.5 %collective-permute-start.10 = (bf16[3,3,1,8192]{3,2,1,0:T(2,128)(2,1)S(1)}, bf16[3,3,1,8192]{3,2,1,0:T(2,128)(2,1)S(1)}, u32[]{:S(2)}, u32[]{:S(2)}) collective-permute-start(bf16[3,3,1,8192]{3,2,1,0:T(2,128)(2,1)S(1)} %get-tuple-element.34), channel_id=1, source_target_pairs={{0,1},{1,2},{2,3},{3,0},{4,5},{5,6},{6,7},{7,4},{8,9},{9,10},{10,1... | collective-permute-start | bytes 442376 | tf_op jit(solution)/shard_map/ppermute | solution.py:23
  80.7 13.9 %collective-permute-start.11 = (bf16[3,3,1,8192]{3,2,1,0:T(2,128)(2,1)S(1)}, bf16[3,3,1,8192]{3,2,1,0:T(2,128)(2,1)S(1)}, u32[]{:S(2)}, u32[]{:S(2)}) collective-permute-start(bf16[3,3,1,8192]{3,2,1,0:T(2,128)(2,1)S(1)} %get-tuple-element.35), channel_id=1, source_target_pairs={{1,0},{2,1},{3,2},{0,3},{5,4},{6,5},{7,6},{4,7},{9,8},{10,9},{11,1... | collective-permute-start | bytes 442376 | tf_op jit(solution)/shard_map/ppermute | solution.py:25
  110.6 11.3 %collective-permute-start.12 = (f32[1,3,4,8192]{3,2,1,0:T(4,128)}, f32[1,3,4,8192]{3,2,1,0:T(4,128)}, u32[]{:S(2)}, u32[]{:S(2)}) collective-permute-start(f32[1,3,4,8192]{3,2,1,0:T(4,128)} %slice.177), channel_id=1, source_target_pairs={{0,32},{32,64},{64,96},{96,128},{128,160},{160,192},{192,224},{224... | collective-permute-start | bytes 1179656 | tf_op jit(solution)/shard_map/ppermute | solution.py:23
  112.3 10.9 %collective-permute-start.13 = (f32[1,3,4,8192]{3,2,1,0:T(4,128)S(1)}, f32[1,3,4,8192]{3,2,1,0:T(4,128)S(1)}, u32[]{:S(2)}, u32[]{:S(2)}) collective-permute-start(f32[1,3,4,8192]{3,2,1,0:T(4,128)S(1)} %slice.179), channel_id=1, source_target_pairs={{32,0},{64,32},{96,64},{128,96},{160,128},{192,160},{224,192},{256... | collective-permute-start | bytes 1179656 | tf_op jit(solution)/shard_map/ppermute | solution.py:25
  123.3 17.7 %collective-permute-start.14 = (f32[5,1,4,8192]{3,2,1,0:T(4,128)S(1)}, f32[5,1,4,8192]{3,2,1,0:T(4,128)S(1)}, u32[]{:S(2)}, u32[]{:S(2)}) collective-permute-start(f32[5,1,4,8192]{3,2,1,0:T(4,128)S(1)} %get-tuple-element.30), channel_id=1, source_target_pairs={{0,4},{4,8},{8,12},{12,16},{16,20},{20,24},{24,28},{28,0},{1,5},{5... | collective-permute-start | bytes 1966088 | tf_op jit(solution)/shard_map/ppermute | solution.py:23
  127.7 21.0 %collective-permute-start.15 = (f32[5,1,4,8192]{3,2,1,0:T(4,128)S(1)}, f32[5,1,4,8192]{3,2,1,0:T(4,128)S(1)}, u32[]{:S(2)}, u32[]{:S(2)}) collective-permute-start(f32[5,1,4,8192]{3,2,1,0:T(4,128)S(1)} %get-tuple-element.31), channel_id=1, source_target_pairs={{4,0},{8,4},{12,8},{16,12},{20,16},{24,20},{28,24},{0,28},{5,1},{9... | collective-permute-start | bytes 1966088 | tf_op jit(solution)/shard_map/ppermute | solution.py:25
  150.5 32.6 %collective-permute-start.16 = (f32[5,5,1,8192]{3,2,1,0:T(1,128)S(1)}, f32[5,5,1,8192]{3,2,1,0:T(1,128)S(1)}, u32[]{:S(2)}, u32[]{:S(2)}) collective-permute-start(f32[5,5,1,8192]{3,2,1,0:T(1,128)S(1)} %get-tuple-element.28), channel_id=1, source_target_pairs={{0,1},{1,2},{2,3},{3,0},{4,5},{5,6},{6,7},{7,4},{8,9},{9,10},{10,1... | collective-permute-start | bytes 2457608 | tf_op jit(solution)/shard_map/ppermute | solution.py:23
  154.9 33.7 %copy-start.11 = (f32[1024,128]{1,0:T(8,128)S(1)}, f32[1024,128]{1,0:T(8,128)}, u32[]{:S(2)}) copy-start(f32[1024,128]{1,0:T(8,128)} %copy-done.9) | copy-start | bytes 1572868
  154.9 33.7 %copy-start.14 = (f32[1024,128]{1,0:T(8,128)S(1)}, f32[1024,128]{1,0:T(8,128)}, u32[]{:S(2)}) copy-start(f32[1024,128]{1,0:T(8,128)} %copy-done.13) | copy-start | bytes 1572868
  154.9 33.7 %copy-start.19 = (bf16[1024,128]{1,0:T(8,128)(2,1)S(1)}, bf16[1024,128]{1,0:T(8,128)(2,1)}, u32[]{:S(2)}) copy-start(bf16[1024,128]{1,0:T(8,128)(2,1)} %copy-done.18) | copy-start | bytes 786436
  155.0 32.6 %collective-permute-start.17 = (f32[5,5,1,8192]{3,2,1,0:T(1,128)S(1)}, f32[5,5,1,8192]{3,2,1,0:T(1,128)S(1)}, u32[]{:S(2)}, u32[]{:S(2)}) collective-permute-start(f32[5,5,1,8192]{3,2,1,0:T(1,128)S(1)} %get-tuple-element.29), channel_id=1, source_target_pairs={{1,0},{2,1},{3,2},{0,3},{5,4},{6,5},{7,6},{4,7},{9,8},{10,9},{11,1... | collective-permute-start | bytes 2457608 | tf_op jit(solution)/shard_map/ppermute | solution.py:25
  206.9 45.6 %copy-start.43 = (f32[128]{0:T(128)S(1)}, f32[128]{0:T(128)}, u32[]{:S(2)}) copy-start(f32[128]{0:T(128)} %param.21) | copy-start | bytes 1540
  206.9 45.6 %copy-start.45 = (f32[1024,128]{1,0:T(8,128)S(1)}, f32[1024,128]{1,0:T(8,128)}, u32[]{:S(2)}) copy-start(f32[1024,128]{1,0:T(8,128)} %copy-done.44) | copy-start | bytes 1572868
  213.9 4.3 %collective-permute-start.18 = (f32[1,3,4,192]{3,2,1,0:T(4,128)S(1)}, f32[1,3,4,192]{3,2,1,0:T(4,128)S(1)}, u32[]{:S(2)}, u32[]{:S(2)}) collective-permute-start(f32[1,3,4,192]{3,2,1,0:T(4,128)S(1)} %slice.195), channel_id=1, source_target_pairs={{0,32},{32,64},{64,96},{96,128},{128,160},{160,192},{192,224},{224... | collective-permute-start | bytes 27656 | tf_op jit(solution)/shard_map/ppermute | solution.py:23
  214.1 6.3 %collective-permute-start.19 = (f32[1,3,4,192]{3,2,1,0:T(4,128)S(1)}, f32[1,3,4,192]{3,2,1,0:T(4,128)S(1)}, u32[]{:S(2)}, u32[]{:S(2)}) collective-permute-start(f32[1,3,4,192]{3,2,1,0:T(4,128)S(1)} %slice.197), channel_id=1, source_target_pairs={{32,0},{64,32},{96,64},{128,96},{160,128},{192,160},{224,192},{256... | collective-permute-start | bytes 27656 | tf_op jit(solution)/shard_map/ppermute | solution.py:25
  220.5 20.6 %collective-permute-start.20 = (f32[5,1,4,192]{3,2,1,0:T(4,128)S(1)}, f32[5,1,4,192]{3,2,1,0:T(4,128)S(1)}, u32[]{:S(2)}, u32[]{:S(2)}) collective-permute-start(f32[5,1,4,192]{3,2,1,0:T(4,128)S(1)} %get-tuple-element.43), channel_id=1, source_target_pairs={{0,4},{4,8},{8,12},{12,16},{16,20},{20,24},{24,28},{28,0},{1,5},{5... | collective-permute-start | bytes 46088 | tf_op jit(solution)/shard_map/ppermute | solution.py:23
  239.1 6.6 %collective-permute-start.21 = (f32[5,1,4,192]{3,2,1,0:T(4,128)S(1)}, f32[5,1,4,192]{3,2,1,0:T(4,128)S(1)}, u32[]{:S(2)}, u32[]{:S(2)}) collective-permute-start(f32[5,1,4,192]{3,2,1,0:T(4,128)S(1)} %get-tuple-element.44), channel_id=1, source_target_pairs={{4,0},{8,4},{12,8},{16,12},{20,16},{24,20},{28,24},{0,28},{5,1},{9... | collective-permute-start | bytes 46088 | tf_op jit(solution)/shard_map/ppermute | solution.py:25
  245.7 8.3 %collective-permute-start.22 = (f32[5,5,1,192]{3,2,1,0:T(1,128)S(1)}, f32[5,5,1,192]{3,2,1,0:T(1,128)S(1)}, u32[]{:S(2)}, u32[]{:S(2)}) collective-permute-start(f32[5,5,1,192]{3,2,1,0:T(1,128)S(1)} %get-tuple-element.36), channel_id=1, source_target_pairs={{0,1},{1,2},{2,3},{3,0},{4,5},{5,6},{6,7},{7,4},{8,9},{9,10},{10,1... | collective-permute-start | bytes 57608 | tf_op jit(solution)/shard_map/ppermute | solution.py:23
  249.2 7.8 %collective-permute-start.23 = (f32[5,5,1,192]{3,2,1,0:T(1,128)S(1)}, f32[5,5,1,192]{3,2,1,0:T(1,128)S(1)}, u32[]{:S(2)}, u32[]{:S(2)}) collective-permute-start(f32[5,5,1,192]{3,2,1,0:T(1,128)S(1)} %get-tuple-element.37), channel_id=1, source_target_pairs={{1,0},{2,1},{3,2},{0,3},{5,4},{6,5},{7,6},{4,7},{9,8},{10,9},{11,1... | collective-permute-start | bytes 57608 | tf_op jit(solution)/shard_map/ppermute | solution.py:25
  (39 other events, 189.5 us)
where the time goes:
time: 259 us; the launch traced here: 258 us
  starting transfers between devices  92.1 us (36%)
  waiting for transfers between devices  83.8 us (32%)
  local copies, waits for them, and re-layouts  33.5 us (13%)
  other arithmetic  27.6 us (11%)
  matrix products  18.8 us (7%)
    ppermute x12, waiting for transfers between devices, padded_2(): lax.ppermute(tail, axis, [(i, (i + 1) % count) for i in range(count)])  54.1 us
    ppermute x12, starting transfers between devices, padded_2(): lax.ppermute(head, axis, [((i + 1) % count, i) for i in range(count)])  46.2 us
    ppermute x12, starting transfers between devices, padded_2(): lax.ppermute(tail, axis, [(i, (i + 1) % count) for i in range(count)])  45.9 us
    ppermute x12, waiting for transfers between devices, padded_2(): lax.ppermute(head, axis, [((i + 1) % count, i) for i in range(count)])  29.7 us
    scatter-add x1, other arithmetic, on_device(): jnp.zeros((padded_count, channels), jnp.float32).at[other_flat]  6.58 us
    scatter-add x1, other arithmetic, on_device(): motion = motion.at[:, other_flat].add(grad_other_pos.reshape(3, -1))  6.48 us
    unnamed x106, local copies, waits for them, and re-layouts  6.47 us
    gather x1, local copies, waits for them, and re-layouts, on_device(): onehot_other = one_hot(ghost_species[other_flat], spec_count)  6.15 us
  transfers between devices with their start and end apart: 24, of which 16 were waited for; matrix products, arithmetic and copies ran while one was open for 4% of the time, Pallas kernels for 0%

commit v1 on v0

v1 whole, which is shorter than its diff:
```python
import math

import jax
import jax.numpy as jnp
from jax import lax
from jax.experimental import pallas as pl
from jax.experimental.pallas import tpu as pltpu
from jax.sharding import PartitionSpec as P

MESH = pl.DeviceIdType.MESH
F32 = jnp.float32
BF16 = jnp.bfloat16
HIGH = lax.Precision.HIGHEST

NEIGH = 8
SLOTS = 64
CUTOFF = 4.0
SHARPNESS = 2.0
NBASIS = 8
CELLS_Z = 2
ATOMS = CELLS_Z * SLOTS
EDGES = ATOMS * NEIGH
WIDTH = 128
PLANE = 256
HALO = 9 * PLANE
GROUP = 16
GROUPS = ATOMS // GROUP
ROOT3 = math.sqrt(3.0)

PARTNERS = ((1, -1), (-1, 1), (1, 1), (-1, -1), (0, 1), (0, -1), (1, 0), (-1, 0))
PART = {0: 0, 1: 1, -1: 2}
ROWS = {0: (0, 128), 1: (128, 64), -1: (192, 64)}
OWN_ROWS = {0: (0, 128), 1: (0, 64), -1: (64, 64)}


def split_bf16(value):
    high = value.astype(BF16)
    return high, (value - high.astype(F32)).astype(BF16)


def dot(a, b, dims=((1,), (0,)), precision=None):
    return lax.dot_general(a, b, (dims, ((), ())), preferred_element_type=F32, precision=precision)


NT = ((1,), (1,))


def sigmoid(value):
    return 0.5 + 0.5 * jnp.tanh(0.5 * value)


def kernel(
    pos_ref,
    spec_ref,
    nbr_ref,
    center_ref,
    neighbor_ref,
    radial_ref,
    mix_ref,
    env_ref,
    update_ref,
    second_ref,
    readout_ref,
    energy_ref,
    force_ref,
    tiles,
    onehot,
    onehot_t,
    table,
    weights,
    act_d,
    mix_d,
    upd_d,
    env_buf,
    diag_a,
    diag_at,
    diag_v,
    latent_buf,
    edge_buf,
    grad_send,
    grad_recv,
    plane_send,
    plane_recv,
    force_tab,
    force_recv,
    force_plane,
    force_plane_recv,
    send_a,
    recv_a,
    send_b,
    recv_b,
    send_c,
    recv_c,
    send_d,
    recv_d,
    send_e,
    recv_e,
    send_f,
    recv_f,
):
    size_x, size_y, size_z = lax.axis_size("gx"), lax.axis_size("gy"), lax.axis_size("gz")
    my_x, my_y, my_z = lax.axis_index("gx"), lax.axis_index("gy"), lax.axis_index("gz")

    def device(dx, dy, dz):
        return (
            lax.rem(my_x + (dx + size_x), size_x),
            lax.rem(my_y + (dy + size_y), size_y),
            lax.rem(my_z + (dz + size_z), size_z),
        )

    def remote(src, dst, send, recv, target):
        return pltpu.make_async_remote_copy(
            src_ref=src, dst_ref=dst, send_sem=send, recv_sem=recv, device_id=target, device_id_type=MESH
        )

    barrier = pltpu.get_barrier_semaphore()
    for dy, dz in PARTNERS:
        pl.semaphore_signal(barrier, inc=1, device_id=device(0, dy, dz), device_id_type=MESH)
    for dx in (-1, 1):
        pl.semaphore_signal(barrier, inc=1, device_id=device(dx, 0, 0), device_id_type=MESH)

    coords = pos_ref[0, 0]
    kinds = spec_ref[0, 0].astype(F32)
    rows = [
        jnp.concatenate([coords[z : z + 1, SLOTS * c : SLOTS * (c + 1)] for z in range(CELLS_Z)], axis=1)
        for c in range(3)
    ]
    rows.append(jnp.concatenate([kinds[z : z + 1, :] for z in range(CELLS_Z)], axis=1))
    own_tile = jnp.concatenate(rows, axis=0)
    tiles[4, 0] = own_tile

    pl.semaphore_wait(barrier, len(PARTNERS) + 2)

    sends = []

    def spread(own_source, yz_dest, columns, sems):
        send_yz, recv_yz, send_x, recv_x = sems
        yz = {}
        for k, (dy, dz) in enumerate(PARTNERS):
            copy = remote(
                own_source(dz), yz_dest(dy, dz), send_yz.at[k], recv_yz.at[k], device(0, -dy, -dz)
            )
            copy.start()
            yz[dy, dz] = copy
        own = forward(columns, 1, "own", send_x, recv_x, 0)
        return yz, own

    def forward(columns, e, part, send_x, recv_x, k):
        copies = []
        for side, dx in enumerate((-1, 1)):
            copy = remote(
                columns(1, e, part),
                columns(dx + 1, e, part),
                send_x.at[2 * k + side],
                recv_x.at[2 * k + side],
                device(-dx, 0, 0),
            )
            copy.start()
            copies.append(copy)
        return copies

    def relay(yz, own, columns, sems):
        send_x, recv_x = sems[2:]
        moved = list(own)
        yz[0, 1].wait_recv()
        yz[0, -1].wait_recv()
        moved += forward(columns, 1, "ends", send_x, recv_x, 1)
        for k, dy in ((2, 1), (3, -1)):
            for dz in (0, 1, -1):
                yz[dy, dz].wait_recv()
            moved += forward(columns, dy + 1, "all", send_x, recv_x, k)
        sends.extend(yz.values())
        sends.extend(moved)
        return moved

    def tile_columns(a, e, part):
        column = tiles.at[3 * a + e]
        return {"own": column.at[0], "ends": column.at[pl.ds(1, 2)], "all": column}[part]

    sems = (send_a, recv_a, send_b.at[0], recv_b.at[0])
    yz, own = spread(
        lambda dz: tiles.at[4, 0], lambda dy, dz: tiles.at[3 + dy + 1, PART[dz]], tile_columns, sems
    )

    codes = nbr_ref[0, 0]
    offset_code = lax.shift_right_logical(codes, 6)
    slot = jnp.bitwise_and(codes, SLOTS - 1)
    column_code = lax.shift_right_logical(offset_code * 171, 9)
    row_z = offset_code - 3 * column_code
    own_z = lax.broadcasted_iota(jnp.int32, codes.shape, 0)
    place = jnp.bitwise_and(row_z + own_z + 3, 3)
    target2 = (column_code * 4 + place) * SLOTS + slot
    step_a = lax.shift_right_logical(column_code * 171, 9)
    step_e = column_code - 3 * step_a

    def flat(value):
        return jnp.concatenate([value[z : z + 1, :] for z in range(CELLS_Z)], axis=1)

    target = flat(target2)
    offsets = [flat(step - 1).astype(F32) for step in (step_a, step_e, row_z)]

    def build_t(t, carry):
        first = pl.multiple_of(t * 128, 128)
        row = lax.broadcasted_iota(jnp.int32, (128, EDGES), 0) + first
        onehot_t[pl.ds(first, 128), :] = (row == target).astype(F32).astype(BF16)
        return carry

    lax.fori_loop(0, HALO // 128, build_t, 0)

    moved_a = relay(yz, own, tile_columns, sems)

    target_rows = jnp.concatenate([target[:, 128 * j : 128 * (j + 1)] for j in range(8)], axis=0)
    target_cols = jnp.transpose(
        jnp.concatenate([target_rows.astype(F32), jnp.zeros((120, 128), F32)], axis=0)
    )
    lane = lax.broadcasted_iota(jnp.int32, (128, 128), 1).astype(F32)
    for j in range(8):
        column = jnp.broadcast_to(target_cols[:, j : j + 1], (128, 128))
        for t in range(HALO // 128):
            onehot[128 * j : 128 * (j + 1), 128 * t : 128 * (t + 1)] = (
                (column == lane + float(128 * t)).astype(F32).astype(BF16)
            )

    weights[...] = jnp.zeros_like(weights)
    weights[0:NBASIS, :] = radial_ref[...].astype(F32)
    spec_count = center_ref.shape[0]
    weights[8 : 8 + spec_count, :] = center_ref[...].astype(F32)
    weights[16 : 16 + spec_count, :] = neighbor_ref[...].astype(F32)
    before_w = weights[...].astype(BF16)

    for copy in moved_a:
        copy.wait_recv()

    half_lane = lax.broadcasted_iota(jnp.int32, (4, 128), 1) < SLOTS
    halves = []
    for p in range(9):
        halves.append(tiles[p, 0])
        halves.append(jnp.where(half_lane, tiles[p, 1], tiles[p, 2]))
    packed = [jnp.concatenate([halves[t], halves[t + 9]], axis=0) for t in range(9)]
    own8 = jnp.concatenate([own_tile, own_tile], axis=0)
    lane8 = lax.broadcasted_iota(jnp.int32, (8, 128), 1)
    others, centers = [], []
    for j in range(8):
        goal = target[:, 128 * j : 128 * (j + 1)]
        spot = jnp.broadcast_to(jnp.bitwise_and(goal, 127), (8, 128))
        which = lax.shift_right_logical(goal, 7)
        late = which >= 9
        which = jnp.broadcast_to(jnp.where(late, which - 9, which), (8, 128))
        found = jnp.zeros((8, 128), F32)
        for t in range(9):
            picked = jnp.take_along_axis(packed[t], spot, axis=1)
            found = jnp.where(which == t, picked, found)
        others.append(jnp.where(jnp.broadcast_to(late, (4, 128)), found[4:8], found[0:4]))
        mine = jnp.take_along_axis(own8, lax.shift_right_logical(lane8, 3) + GROUP * j, axis=1)
        centers.append(mine[0:4])
    other = jnp.concatenate(others, axis=1)
    center = jnp.concatenate(centers, axis=1)

    d_x, d_y, d_z = (offsets[c] + (other[c : c + 1] - center[c : c + 1]) for c in range(3))
    distance = jnp.sqrt(d_x * d_x + d_y * d_y + d_z * d_z)
    inverse = 1.0 / distance
    u_x, u_y, u_z = d_x * inverse, d_y * inverse, d_z * inverse
    angular = [
        jnp.ones_like(u_x),
        u_x,
        u_y,
        u_z,
        ROOT3 * u_x * u_y,
        ROOT3 * u_y * u_z,
        0.5 * (3.0 * u_z * u_z - 1.0),
        ROOT3 * u_x * u_z,
        0.5 * ROOT3 * (u_x * u_x - u_y * u_y),
    ]
    ratio = distance * (1.0 / CUTOFF)
    inside = 1.0 - ratio * ratio
    index8 = lax.broadcasted_iota(jnp.int32, (8, EDGES), 0)
    mu = (index8.astype(F32) + 0.5) * (CUTOFF / NBASIS)
    apart = distance - mu
    bell = jnp.exp(-SHARPNESS * apart * apart)
    basis = bell * (inside * inside)
    basis_d = bell * (-2.0 * SHARPNESS * apart * (inside * inside) - ratio * inside)
    hot_center = (index8.astype(F32) == center[3:4]).astype(F32)
    hot_other = (index8.astype(F32) == other[3:4]).astype(F32)
    features = jnp.concatenate([basis, hot_center, hot_other], axis=0)
    features = jnp.transpose(features).astype(BF16)

    before = dot(features, before_w)
    gate = sigmoid(before)
    act = before * gate
    act_d[...] = gate + act * (1.0 - gate)
    mixed = dot(act.astype(BF16), mix_ref[...])
    gate = sigmoid(mixed)
    latent = mixed * gate
    mix_d[...] = gate + latent * (1.0 - gate)
    latent_buf[...] = latent
    env_buf[...] = dot(latent.astype(BF16), env_ref[...]).astype(BF16)

    group_mask = (
        lax.shift_right_logical(lax.broadcasted_iota(jnp.int32, (GROUP, 128), 1), 3)
        == lax.broadcasted_iota(jnp.int32, (GROUP, 128), 0)
    ).astype(F32)
    zero = {n: jnp.zeros((GROUP * n, WIDTH), BF16) for n in (1, 3, 5)}
    update_w = update_ref[...]
    for j in range(GROUPS):
        span = slice(128 * j, 128 * (j + 1))
        spread_y = jnp.concatenate([angular[m][:, span] * group_mask for m in range(9)], axis=0)
        diag_a[j] = spread_y.astype(BF16)
        diag_at[j] = jnp.transpose(spread_y).astype(BF16)
        value = (dot(diag_a[j], env_buf[span, :]) * (1.0 / NEIGH)).astype(BF16)
        diag_v[j] = jnp.concatenate(
            [
                jnp.concatenate([value[0:16], zero[1], zero[1]], axis=1),
                jnp.concatenate([zero[3], value[16:64], zero[3]], axis=1),
                jnp.concatenate([zero[5], zero[5], value[64:144]], axis=1),
            ],
            axis=0,
        )
        invariant = dot(diag_at[j], diag_v[j]).astype(BF16)
        summed = latent_buf[span, :] + dot(invariant, update_w)
        gate = sigmoid(summed)
        edge = summed * gate
        upd_d[span, :] = gate + edge * (1.0 - gate)
        edge_buf[span, :] = edge

    members = (
        lax.shift_right_logical(lax.broadcasted_iota(jnp.int32, (ATOMS, EDGES), 1), 3)
        == lax.broadcasted_iota(jnp.int32, (ATOMS, EDGES), 0)
    ).astype(F32).astype(BF16)
    high, low = split_bf16(edge_buf[...])
    table[4, 0:ATOMS, :] = ((dot(members, high) + dot(members, low)) * (1.0 / NEIGH)).astype(BF16)

    def table_columns(a, e, part):
        column = table.at[3 * a + e]
        return {"own": column.at[pl.ds(0, 128)], "ends": column.at[pl.ds(128, 128)], "all": column}[part]

    sems = (send_c, recv_c, send_b.at[1], recv_b.at[1])
    yz, own = spread(
        lambda dz: table.at[4, pl.ds(*OWN_ROWS[dz])],
        lambda dy, dz: table.at[3 + dy + 1, pl.ds(*ROWS[dz])],
        table_columns,
        sems,
    )
    moved_c = relay(yz, own, table_columns, sems)
    middle = jnp.concatenate([table[3], table[4], table[5]], axis=0)
    other_latent = dot(onehot[:, 768:1536], middle)
    for copy in moved_c:
        copy.wait_recv()
    before_plane = jnp.concatenate([table[0], table[1], table[2]], axis=0)
    after_plane = jnp.concatenate([table[6], table[7], table[8]], axis=0)
    other_latent = other_latent + dot(onehot[:, 0:768], before_plane) + dot(onehot[:, 1536:2304], after_plane)

    edge = edge_buf[...]
    product = (edge * other_latent).astype(BF16)
    second_w = second_ref[...]
    readout = readout_ref[...]
    hidden_in = dot(product, second_w)
    gate = sigmoid(hidden_in)
    hidden = hidden_in * gate
    hidden_g = (readout * (gate + hidden * (1.0 - gate))).astype(BF16)
    product_g = dot(hidden_g, second_w, NT).astype(BF16).astype(F32)
    other_g = (product_g * edge).astype(BF16)
    edge_buf[...] = product_g * other_latent

    moved_x = {}
    for side, dx in enumerate((-1, 1)):
        for e in (0, 2, 1):
            first = 256 * (3 * (dx + 1) + e)
            grad_send[side, e] = dot(onehot_t[first : first + 256, :], other_g).astype(BF16)
            copy = remote(
                grad_send.at[side, e],
                grad_recv.at[side, e],
                send_d.at[3 * side + e],
                recv_d.at[3 * side + e],
                device(dx, 0, 0),
            )
            copy.start()
            moved_x[side, e] = copy
    plane_sum = {e: dot(onehot_t[768 + 256 * e : 1024 + 256 * e, :], other_g) for e in range(3)}

    high, low = split_bf16(hidden * readout)
    atom_terms = dot(members, high) + dot(members, low)
    energy = dot(jnp.ones((8, WIDTH), F32), atom_terms, NT, HIGH)
    energy_ref[0, 0] = jnp.concatenate(
        [energy[0:1, SLOTS * z : SLOTS * (z + 1)] for z in range(CELLS_Z)], axis=0
    )

    moved_yz = {}
    for e in (0, 2, 1):
        moved_x[0, e].wait_recv()
        moved_x[1, e].wait_recv()
        plane_sum[e] = plane_sum[e] + grad_recv[0, e].astype(F32) + grad_recv[1, e].astype(F32)
        plane_send[e] = plane_sum[e].astype(BF16)
        for k, (dy, dz) in enumerate(PARTNERS):
            if dy == e - 1:
                rows_send = pl.ds(*ROWS[dz])
                copy = remote(
                    plane_send.at[e, rows_send],
                    plane_recv.at[k, pl.ds(0, ROWS[dz][1])],
                    send_c.at[8 + k],
                    recv_c.at[8 + k],
                    device(0, dy, dz),
                )
                copy.start()
                moved_yz[k] = copy
    for copy in moved_yz.values():
        copy.wait_recv()
    sends.extend(moved_x.values())
    sends.extend(moved_yz.values())
    parts = {0: plane_sum[1][0:128]}
    for k, (dy, dz) in enumerate(PARTNERS):
        got = plane_recv[k, 0 : ROWS[dz][1], :].astype(F32)
        parts[dz] = got if dz not in parts else parts[dz] + got
    owned = parts[0] + jnp.concatenate([parts[1], parts[-1]], axis=0)

    owned_edges = jnp.broadcast_to((owned * (1.0 / NEIGH))[:, None, :], (ATOMS, NEIGH, WIDTH)).reshape(EDGES, WIDTH)
    summed_g = (edge_buf[...] + owned_edges) * upd_d[...]
    edge_buf[...] = summed_g
    invariant_g = dot(summed_g.astype(BF16), update_w, NT).astype(BF16)
    angular_g = [[] for _ in range(9)]
    for j in range(GROUPS):
        span = slice(128 * j, 128 * (j + 1))
        inv_g = invariant_g[span, :]
        wide = dot(diag_a[j], inv_g)
        value_g = (
            jnp.concatenate([wide[0:16, 0:128], wide[16:64, 128:256], wide[64:144, 256:384]], axis=0)
            * (1.0 / NEIGH)
        ).astype(BF16)
        act_env = env_buf[span, :]
        all_g = dot(diag_v[j], inv_g, NT) + dot(value_g, act_env, NT)
        for m in range(9):
            angular_g[m].append(
                jnp.sum(all_g[GROUP * m : GROUP * (m + 1)] * group_mask, axis=0, keepdims=True)
            )
        latent_buf[span, :] = dot(diag_at[j], value_g)
    latent_g = dot(latent_buf[...].astype(BF16), env_ref[...], NT).astype(BF16).astype(F32)
    mixed_g = ((edge_buf[...] + latent_g) * mix_d[...]).astype(BF16)
    act_g = dot(mixed_g, mix_ref[...], NT).astype(BF16).astype(F32)
    before_g = (act_g * act_d[...]).astype(BF16)
    basis_g = dot(radial_ref[...], before_g, NT).astype(BF16).astype(F32)

    distance_g = jnp.sum(basis_g * basis_d, axis=0, keepdims=True)
    g = [jnp.concatenate(parts_m, axis=1) for parts_m in angular_g]
    gu_x = g[1] + ROOT3 * (u_y * g[4] + u_z * g[7] + u_x * g[8])
    gu_y = g[2] + ROOT3 * (u_x * g[4] + u_z * g[5] - u_y * g[8])
    gu_z = g[3] + ROOT3 * (u_y * g[5] + u_x * g[7]) + 3.0 * u_z * g[6]
    along = distance_g - inverse * (u_x * gu_x + u_y * gu_y + u_z * gu_z)
    pull = [-(gu * inverse + u * along) for gu, u in ((gu_x, u_x), (gu_y, u_y), (gu_z, u_z))]
    pull4 = jnp.concatenate(pull + [jnp.zeros_like(u_x)], axis=0)
    high = pull4.astype(BF16).astype(F32)
    pull8 = jnp.concatenate([high, pull4 - high], axis=0).astype(BF16)

    def scatter(first, count):
        both = dot(pull8, onehot_t[first : first + count, :], NT)
        return both[0:4] + both[4:8]

    moved_f = []
    for side, dx in enumerate((-1, 1)):
        a = dx + 1
        got = scatter(768 * a, 768)
        for i in range(6):
            force_tab[side, i] = got[:, 128 * i : 128 * (i + 1)]
        copy = remote(
            force_tab.at[side], force_recv.at[side], send_e.at[side], recv_e.at[side], device(dx, 0, 0)
        )
        copy.start()
        moved_f.append(copy)
    middle_f = scatter(768, 768)
    both = dot(pull8, members, NT)
    own_f = both[0:4] + both[4:8]
    for copy in moved_f:
        copy.wait_recv()
    for i in range(6):
        force_plane[i] = middle_f[:, 128 * i : 128 * (i + 1)] + force_recv[0, i] + force_recv[1, i]
    moved_g = []
    for k, (dy, dz) in enumerate(PARTNERS):
        copy = remote(
            force_plane.at[2 * (dy + 1) + (1 if dz else 0)],
            force_plane_recv.at[k],
            send_f.at[k],
            recv_f.at[k],
            device(0, dy, dz),
        )
        copy.start()
        moved_g.append(copy)
    for copy in moved_g:
        copy.wait_recv()
    sends.extend(moved_f)
    sends.extend(moved_g)
    total = force_plane[2] - own_f
    ends = {}
    for k, (dy, dz) in enumerate(PARTNERS):
        got = force_plane_recv[k]
        if dz == 0:
            total = total + got
        else:
            ends[dz] = got if dz not in ends else ends[dz] + got
    total = total + jnp.where(half_lane, ends[1], ends[-1])
    force_ref[0, 0] = jnp.concatenate(
        [
            jnp.concatenate([total[c : c + 1, SLOTS * z : SLOTS * (z + 1)] for c in range(3)], axis=1)
            for z in range(CELLS_Z)
        ],
        axis=0,
    )
    for copy in sends:
        copy.wait_send()


def on_device(
    positions,
    species,
    neighbors,
    center_table,
    neighbor_table,
    radial_weight,
    mix_weight,
    env_weight,
    update_weight,
    second_weight,
    readout,
):
    dma = pltpu.SemaphoreType.DMA
    vmem = pltpu.VMEM
    cells = positions.shape[:3]
    return pl.pallas_call(
        kernel,
        out_shape=(
            jax.ShapeDtypeStruct((*cells, SLOTS), F32),
            jax.ShapeDtypeStruct((*cells, 3 * SLOTS), F32),
        ),
        in_specs=[pl.BlockSpec(memory_space=pltpu.VMEM)] * 11,
        out_specs=[pl.BlockSpec(memory_space=pltpu.VMEM)] * 2,
        scratch_shapes=[
            vmem((9, 3, 4, 128), F32),
            vmem((EDGES, HALO), BF16),
            vmem((HALO, EDGES), BF16),
            vmem((9, PLANE, WIDTH), BF16),
            vmem((24, WIDTH), F32),
            vmem((EDGES, WIDTH), F32),
            vmem((EDGES, WIDTH), F32),
            vmem((EDGES, WIDTH), F32),
            vmem((EDGES, WIDTH), BF16),
            vmem((GROUPS, 9 * GROUP, 128), BF16),
            vmem((GROUPS, 128, 9 * GROUP), BF16),
            vmem((GROUPS, 9 * GROUP, 3 * WIDTH), BF16),
            vmem((EDGES, WIDTH), F32),
            vmem((EDGES, WIDTH), F32),
            vmem((2, 3, PLANE, WIDTH), BF16),
            vmem((2, 3, PLANE, WIDTH), BF16),
            vmem((3, PLANE, WIDTH), BF16),
            vmem((8, 128, WIDTH), BF16),
            vmem((2, 6, 4, 128), F32),
            vmem((2, 6, 4, 128), F32),
            vmem((6, 4, 128), F32),
            vmem((8, 4, 128), F32),
            dma((8,)),
            dma((8,)),
            dma((2, 8)),
            dma((2, 8)),
            dma((16,)),
            dma((16,)),
            dma((6,)),
            dma((6,)),
            dma((2,)),
            dma((2,)),
            dma((8,)),
            dma((8,)),
        ],
        compiler_params=pltpu.CompilerParams(collective_id=0, has_side_effects=True),
    )(
        positions,
        species,
        neighbors,
        center_table,
        neighbor_table,
        radial_weight,
        mix_weight,
        env_weight,
        update_weight,
        second_weight,
        readout.reshape(1, WIDTH),
    )


def solution(mesh):
    placed = (
        P("gx", "gy", "gz", None),
        P("gx", "gy", "gz", None),
        P("gx", "gy", "gz", None),
        P(),
        P(),
        P(),
        P(),
        P(),
        P(),
        P(),
        P(),
    )
    return jax.shard_map(
        on_device,
        mesh=mesh,
        in_specs=placed,
        out_specs=(P("gx", "gy", "gz", None), P("gx", "gy", "gz", None)),
        check_vma=False,
    )
```

time: 259 us -> 65.6 us (0.25)
  the two profiles are of different devices: /device:TPU:28 before, /device:TPU:1 now
where the time goes in v1:
time: 65.6 us; the launch traced here: 65.4 us
  Pallas kernels  63 us (96%)
  local copies, waits for them, and re-layouts  1.76 us (3%)
  between operations  0.66 us (1%)
    pallas_call x1, Pallas kernels, on_device(): pl.pallas_call(kernel, out_shape=(jax.ShapeDtypeStruct((*cells, SLOTS), F...  63 us
    unnamed x6, local copies, waits for them, and re-layouts  1.76 us

profile of v1, /device:TPU:1, one launch (start us, length us, event | category | flops | bytes accessed | tf_op | source)
XLA Modules:
  0.0 65.4 jit_solution(12273695695860199932)
XLA Ops:
  0.6 63.0 %shard_map.122 = (f32[1,1,2,64]{3,2,1,0:T(2,128)}, f32[1,1,2,192]{3,2,1,0:T(2,128)}) custom-call(f32[1,1,2,192]{3,2,1,0:T(2,128)} %pos_ref.1, s32[1,1,2,64]{3,2,1,0:T(2,128)} %spec_ref.1, s32[1,1,2,512]{3,2,1,0:T(2,128)} %nbr_ref.1, bf16[5,128]{1,0:T(8,128)(2,1)} %center_ref.1, bf16[5,128]{1,0:T(8,128)(2,1)} %neighbor_ref.1, bf16[8,128]{1,0:T(8,128)(2,1)} %radial_ref.1, ...), custom_call_target="tpu_custom_call" | custom-call | tf_op jit(solution)/shard_map/pallas_call | solution.py:525
  63.7 0.0 copy-start.1
  63.7 0.0 copy-start
  63.7 0.6 copy-done.1
  64.3 0.6 copy.15
  64.8 0.0 copy-done
  64.9 0.6 copy.16
Async XLA Ops:
  63.7 0.6 copy-start.1
  63.7 1.2 %copy-start = (f32[1,1,2,192]{3,2,1,0:T(2,128)S(1)}, f32[1,1,2,192]{3,2,1,0:T(2,128)}, u32[]{:S(2)}) copy-start(f32[1,1,2,192]{3,2,1,0:T(2,128)} %get-tuple-element.5) | copy-start | bytes 4612

commit v2 on v1

v2 whole, which is shorter than its diff:
```python
import itertools
import math

import jax
import jax.numpy as jnp
from jax import lax
from jax.experimental import pallas as pl
from jax.experimental.pallas import tpu as pltpu
from jax.sharding import PartitionSpec as P

MESH = pl.DeviceIdType.MESH
F32 = jnp.float32
BF16 = jnp.bfloat16
HIGH = lax.Precision.HIGHEST

NEIGH = 8
SLOTS = 64
CUTOFF = 4.0
SHARPNESS = 2.0
NBASIS = 8
CELLS_Z = 2
ATOMS = CELLS_Z * SLOTS
EDGES = ATOMS * NEIGH
WIDTH = 128
PLANE = 256
LEVEL = 3 * PLANE
GROUP = 16
GROUPS = ATOMS // GROUP
ROOT3 = math.sqrt(3.0)

PARTNERS = ((1, -1), (-1, 1), (1, 1), (-1, -1), (0, 1), (0, -1), (1, 0), (-1, 0))
AROUND = sorted(
    (d for d in itertools.product((-1, 0, 1), repeat=3) if any(d)), key=lambda d: -sum(abs(c) for c in d)
)
PART = {0: 0, 1: 1, -1: 2}
ROWS = {0: (0, 128), 1: (128, 64), -1: (192, 64)}
OWN_ROWS = {0: (0, 128), 1: (0, 64), -1: (64, 64)}


def split_bf16(value):
    high = value.astype(BF16)
    return high, (value - high.astype(F32)).astype(BF16)


def dot(a, b, dims=((1,), (0,)), precision=None):
    return lax.dot_general(a, b, (dims, ((), ())), preferred_element_type=F32, precision=precision)


NT = ((1,), (1,))


def sigmoid(value):
    return 0.5 + 0.5 * jnp.tanh(0.5 * value)


def kernel(
    pos_in,
    spec_in,
    nbr_in,
    center_in,
    neighbor_in,
    radial_in,
    mix_in,
    env_in,
    update_in,
    second_in,
    readout_in,
    out_ref,
    pos_ref,
    spec_ref,
    nbr_ref,
    center_ref,
    neighbor_ref,
    radial_ref,
    mix_ref,
    env_ref,
    update_ref,
    second_ref,
    readout_ref,
    load_sem,
    tiles,
    onehot,
    onehot_t,
    target_col,
    level_col,
    table,
    weights,
    act_d,
    mix_d,
    upd_d,
    env_buf,
    diag_a,
    diag_at,
    value_0,
    value_1,
    value_2,
    mixed_0,
    mixed_1,
    mixed_2,
    summed_b,
    latent_buf,
    edge_buf,
    grad_send,
    grad_recv,
    plane_send,
    plane_recv,
    force_tab,
    force_recv,
    send_a,
    recv_a,
    send_c,
    recv_c,
    send_x,
    recv_x,
    send_d,
    recv_d,
    send_f,
    recv_f,
):
    size_x, size_y, size_z = lax.axis_size("gx"), lax.axis_size("gy"), lax.axis_size("gz")
    my_x, my_y, my_z = lax.axis_index("gx"), lax.axis_index("gy"), lax.axis_index("gz")

    def device(dx, dy, dz):
        return (
            lax.rem(my_x + (dx + size_x), size_x),
            lax.rem(my_y + (dy + size_y), size_y),
            lax.rem(my_z + (dz + size_z), size_z),
        )

    def remote(src, dst, send, recv, target):
        return pltpu.make_async_remote_copy(
            src_ref=src, dst_ref=dst, send_sem=send, recv_sem=recv, device_id=target, device_id_type=MESH
        )

    barrier = pltpu.get_barrier_semaphore()
    for step in AROUND:
        pl.semaphore_signal(barrier, inc=1, device_id=device(*step), device_id_type=MESH)

    sources = (
        pos_in, spec_in, nbr_in, center_in, neighbor_in, radial_in, mix_in, env_in, update_in, second_in, readout_in
    )
    places = (
        pos_ref, spec_ref, nbr_ref, center_ref, neighbor_ref, radial_ref, mix_ref, env_ref, update_ref, second_ref,
        readout_ref,
    )
    loads = [pltpu.make_async_copy(src, dst, load_sem.at[k]) for k, (src, dst) in enumerate(zip(sources, places))]
    for load in loads:
        load.start()
    loads[0].wait()
    loads[1].wait()

    coords = pos_ref[0, 0]
    kinds = spec_ref[0, 0].astype(F32)
    rows = [
        jnp.concatenate([coords[z : z + 1, SLOTS * c : SLOTS * (c + 1)] for z in range(CELLS_Z)], axis=1)
        for c in range(3)
    ]
    rows.append(jnp.concatenate([kinds[z : z + 1, :] for z in range(CELLS_Z)], axis=1))
    own_tile = jnp.concatenate(rows, axis=0)
    tiles[4, 0] = own_tile

    pl.semaphore_wait(barrier, len(AROUND))

    sends = []

    far_side = lax.rem(my_x, 2)
    sides = (far_side, 1 - far_side)

    def forward(source, dest, send, recv, k):
        copies = []
        for side in sides[::-1]:
            copy = remote(
                source,
                dest(3 * (2 * side)),
                send.at[2 * k + side],
                recv.at[2 * k + side],
                device(1 - 2 * side, 0, 0),
            )
            copy.start()
            copies.append(copy)
        sends.extend(copies)
        return copies

    moved_a = []
    for k, (dx, dy, dz) in enumerate(AROUND):
        copy = remote(
            tiles.at[4, 0], tiles.at[3 * dx + dy + 4, PART[dz]], send_a.at[k], recv_a.at[k], device(-dx, -dy, -dz)
        )
        copy.start()
        moved_a.append(copy)
    sends.extend(moved_a)

    loads[2].wait()
    codes = nbr_ref[0, 0]
    offset_code = lax.shift_right_logical(codes, 6)
    slot = jnp.bitwise_and(codes, SLOTS - 1)
    column_code = lax.shift_right_logical(offset_code * 171, 9)
    row_z = offset_code - 3 * column_code
    own_z = lax.broadcasted_iota(jnp.int32, codes.shape, 0)
    place = jnp.bitwise_and(row_z + own_z + 3, 3)
    step_a = lax.shift_right_logical(column_code * 171, 9)
    step_e = column_code - 3 * step_a

    def flat(value):
        return jnp.concatenate([value[z : z + 1, :] for z in range(CELLS_Z)], axis=1)

    target = flat((step_e * 4 + place) * SLOTS + slot)
    level = flat(step_a)
    offsets = [flat(step - 1).astype(F32) for step in (step_a, step_e, row_z)]

    for load in loads[3:]:
        load.wait()
    weights[...] = jnp.zeros_like(weights)
    weights[0:NBASIS, :] = radial_ref[...].astype(F32)
    spec_count = center_ref.shape[0]
    weights[8 : 8 + spec_count, :] = center_ref[...].astype(F32)
    weights[16 : 16 + spec_count, :] = neighbor_ref[...].astype(F32)
    before_w = weights[...].astype(BF16)

    for copy in moved_a:
        copy.wait_recv()

    half_lane = lax.broadcasted_iota(jnp.int32, (4, 128), 1) < SLOTS
    halves = []
    for p in range(9):
        halves.append(tiles[p, 0])
        halves.append(jnp.where(half_lane, tiles[p, 1], tiles[p, 2]))
    packed = [jnp.concatenate([halves[t], halves[t + 9]], axis=0) for t in range(9)]
    own8 = jnp.concatenate([own_tile, own_tile], axis=0)
    lane8 = lax.broadcasted_iota(jnp.int32, (8, 128), 1)
    others, centers = [], []
    for j in range(8):
        goal = (target + LEVEL * level)[:, 128 * j : 128 * (j + 1)]
        spot = jnp.broadcast_to(jnp.bitwise_and(goal, 127), (8, 128))
        which = lax.shift_right_logical(goal, 7)
        late = which >= 9
        which = jnp.broadcast_to(jnp.where(late, which - 9, which), (8, 128))
        found = jnp.zeros((8, 128), F32)
        for t in range(9):
            picked = jnp.take_along_axis(packed[t], spot, axis=1)
            found = jnp.where(which == t, picked, found)
        others.append(jnp.where(jnp.broadcast_to(late, (4, 128)), found[4:8], found[0:4]))
        mine = jnp.take_along_axis(own8, lax.shift_right_logical(lane8, 3) + GROUP * j, axis=1)
        centers.append(mine[0:4])
    other = jnp.concatenate(others, axis=1)
    center = jnp.concatenate(centers, axis=1)

    d_x, d_y, d_z = (offsets[c] + (other[c : c + 1] - center[c : c + 1]) for c in range(3))
    distance = jnp.sqrt(d_x * d_x + d_y * d_y + d_z * d_z)
    inverse = 1.0 / distance
    u_x, u_y, u_z = d_x * inverse, d_y * inverse, d_z * inverse
    angular = [
        jnp.ones_like(u_x),
        u_x,
        u_y,
        u_z,
        ROOT3 * u_x * u_y,
        ROOT3 * u_y * u_z,
        0.5 * (3.0 * u_z * u_z - 1.0),
        ROOT3 * u_x * u_z,
        0.5 * ROOT3 * (u_x * u_x - u_y * u_y),
    ]
    ratio = distance * (1.0 / CUTOFF)
    inside = 1.0 - ratio * ratio
    index8 = lax.broadcasted_iota(jnp.int32, (8, EDGES), 0)
    mu = (index8.astype(F32) + 0.5) * (CUTOFF / NBASIS)
    apart = distance - mu
    bell = jnp.exp(-SHARPNESS * apart * apart)
    basis = bell * (inside * inside)
    basis_d = bell * (-2.0 * SHARPNESS * apart * (inside * inside) - ratio * inside)
    hot_center = (index8.astype(F32) == center[3:4]).astype(F32)
    hot_other = (index8.astype(F32) == other[3:4]).astype(F32)
    features = jnp.concatenate([basis, hot_center, hot_other], axis=0)
    features = jnp.transpose(features).astype(BF16)

    group_mask = (
        lax.shift_right_logical(lax.broadcasted_iota(jnp.int32, (GROUP, 128), 1), 3)
        == lax.broadcasted_iota(jnp.int32, (GROUP, 128), 0)
    ).astype(F32)
    members = (
        lax.shift_right_logical(lax.broadcasted_iota(jnp.int32, (ATOMS, EDGES), 1), 3)
        == lax.broadcasted_iota(jnp.int32, (ATOMS, EDGES), 0)
    ).astype(F32).astype(BF16)
    levels = ((0, 1), (1, 4), (4, 9))
    update_w = [update_ref[WIDTH * l : WIDTH * (l + 1), :] for l in range(3)]

    def gathered(buffers, j):
        return jnp.concatenate(
            [
                buffer[GROUP * (stop - start) * j : GROUP * (stop - start) * (j + 1), :]
                for buffer, (start, stop) in zip(buffers, levels)
            ],
            axis=0,
        )

    def placed(buffers, j, value):
        for buffer, (start, stop) in zip(buffers, levels):
            rows_l = GROUP * (stop - start)
            buffer[rows_l * j : rows_l * (j + 1), :] = value[GROUP * start : GROUP * stop]

    values = (value_0, value_1, value_2)
    mixes = (mixed_0, mixed_1, mixed_2)
    half_edges = EDGES // CELLS_Z
    half_groups = GROUPS // CELLS_Z
    yz = {}
    moved_c = []
    for z in range(CELLS_Z):
        block = slice(half_edges * z, half_edges * (z + 1))
        before = dot(features[block, :], before_w)
        gate = sigmoid(before)
        act = before * gate
        act_d[block, :] = gate + act * (1.0 - gate)
        mixed = dot(act.astype(BF16), mix_ref[...])
        gate = sigmoid(mixed)
        latent = mixed * gate
        mix_d[block, :] = gate + latent * (1.0 - gate)
        env_buf[block, :] = dot(latent.astype(BF16), env_ref[...]).astype(BF16)
        for j in range(half_groups * z, half_groups * (z + 1)):
            span = slice(128 * j, 128 * (j + 1))
            spread_y = jnp.concatenate([angular[m][:, span] * group_mask for m in range(9)], axis=0)
            diag_a[j] = spread_y.astype(BF16)
            diag_at[j] = jnp.transpose(spread_y).astype(BF16)
            placed(values, j, (dot(diag_a[j], env_buf[span, :]) * (1.0 / NEIGH)).astype(BF16))
        for value, mixed_l, weight, (start, stop) in zip(values, mixes, update_w, levels):
            rows_l = GROUP * (stop - start) * half_groups
            span = slice(rows_l * z, rows_l * (z + 1))
            mixed_l[span, :] = dot(value[span, :], weight).astype(BF16)
        update = jnp.concatenate(
            [dot(diag_at[j], gathered(mixes, j)) for j in range(half_groups * z, half_groups * (z + 1))], axis=0
        )
        summed = latent + update
        gate = sigmoid(summed)
        edge = summed * gate
        upd_d[block, :] = gate + edge * (1.0 - gate)
        edge_buf[block, :] = edge
        high, low = split_bf16(edge)
        mine = members[0:SLOTS, 0:half_edges]
        own_rows = pl.ds(SLOTS * z, SLOTS)
        table[4, SLOTS * z : SLOTS * (z + 1), :] = ((dot(mine, high) + dot(mine, low)) * (1.0 / NEIGH)).astype(BF16)
        for k, (dy, dz) in enumerate(PARTNERS):
            if dz == (-1 if z == 0 else 1):
                continue
            rows_there = own_rows if dz == 0 else pl.ds(*ROWS[dz])
            copy = remote(
                table.at[4, own_rows],
                table.at[4 + dy, rows_there],
                send_c.at[k + 8 * z],
                recv_c.at[k + 8 * z],
                device(0, -dy, -dz),
            )
            copy.start()
            yz[dy, dz, z] = copy
        moved_c.append(
            forward(
                table.at[4, own_rows], lambda a, own_rows=own_rows: table.at[a + 1, own_rows], send_x, recv_x, z
            )
        )
    sends.extend(yz.values())

    row_kinds = [target[:, 128 * j : 128 * (j + 1)].astype(F32) for j in range(8)]
    row_kinds += [level[:, 128 * j : 128 * (j + 1)].astype(F32) for j in range(8)]
    columns = jnp.transpose(jnp.concatenate(row_kinds + [jnp.zeros((112, 128), F32)], axis=0))
    for j in range(8):
        target_col[j] = jnp.broadcast_to(columns[:, j : j + 1], (128, 128))
        level_col[128 * j : 128 * (j + 1), :] = jnp.broadcast_to(columns[:, 8 + j : 9 + j], (128, 128))

    def build(j, carry):
        first = pl.multiple_of(j * 128, 128)
        lane = lax.broadcasted_iota(jnp.int32, (128, 128), 1).astype(F32)
        column = target_col[j]
        for t in range(LEVEL // 128):
            onehot[pl.ds(first, 128), 128 * t : 128 * (t + 1)] = (
                (column == lane + float(128 * t)).astype(F32).astype(BF16)
            )
        return carry

    lax.fori_loop(0, GROUPS, build, 0)

    def build_t(t, carry):
        first = pl.multiple_of(t * 128, 128)
        row = lax.broadcasted_iota(jnp.int32, (128, EDGES), 0) + first
        onehot_t[pl.ds(first, 128), :] = (row == target).astype(F32).astype(BF16)
        return carry

    lax.fori_loop(0, LEVEL // 128, build_t, 0)

    ends = pl.ds(128, 128)
    pair = pl.ds(0, 128)
    yz[0, 1, 0].wait_recv()
    yz[0, -1, 1].wait_recv()
    moved_c.append(forward(table.at[4, ends], lambda a: table.at[a + 1, ends], send_x, recv_x, 2))
    for k, dy in ((3, 1), (5, -1)):
        yz[dy, 0, 0].wait_recv()
        yz[dy, 0, 1].wait_recv()
        moved_c.append(forward(table.at[4 + dy, pair], lambda a, dy=dy: table.at[a + 1 + dy, pair], send_x, recv_x, k))
        yz[dy, 1, 0].wait_recv()
        yz[dy, -1, 1].wait_recv()
        moved_c.append(
            forward(table.at[4 + dy, ends], lambda a, dy=dy: table.at[a + 1 + dy, ends], send_x, recv_x, k + 1)
        )
    here = dot(onehot[...], jnp.concatenate([table[3], table[4], table[5]], axis=0))
    beside = jnp.zeros((EDGES, 2 * WIDTH), F32)
    for e, chunks in ((1, (0, 1, 2)), (2, (3, 4)), (0, (5, 6))):
        for c in chunks:
            for copy in moved_c[c]:
                copy.wait_recv()
        pair_e = jnp.concatenate([table[e], table[6 + e]], axis=1)
        beside = beside + dot(onehot[:, PLANE * e : PLANE * (e + 1)], pair_e)
    levels_e = level_col[...]
    other_latent = jnp.where(
        levels_e == 1.0, here, jnp.where(levels_e == 0.0, beside[:, 0:WIDTH], beside[:, WIDTH : 2 * WIDTH])
    )

    edge = edge_buf[...]
    product = (edge * other_latent).astype(BF16)
    second_w = second_ref[...]
    readout = readout_ref[...]
    hidden_in = dot(product, second_w)
    gate = sigmoid(hidden_in)
    hidden = hidden_in * gate
    hidden_g = (readout * (gate + hidden * (1.0 - gate))).astype(BF16)
    product_g = dot(hidden_g, second_w, NT).astype(BF16).astype(F32)
    other_g = product_g * edge
    none = jnp.zeros_like(other_g)
    beside_g = jnp.concatenate(
        [jnp.where(levels_e == 0.0, other_g, none), jnp.where(levels_e == 2.0, other_g, none)], axis=1
    ).astype(BF16)
    here_g = jnp.where(levels_e == 1.0, other_g, none).astype(BF16)
    edge_buf[...] = product_g * other_latent

    moved_x = {}
    for e in (0, 2, 1):
        grads = dot(onehot_t[PLANE * e : PLANE * (e + 1), :], beside_g).astype(BF16)
        grad_send[0, e] = grads[:, 0:WIDTH]
        grad_send[1, e] = grads[:, WIDTH : 2 * WIDTH]
        for order, side in enumerate(sides):
            copy = remote(
                grad_send.at[side, e],
                grad_recv.at[side, e],
                send_d.at[3 * side + e],
                recv_d.at[3 * side + e],
                device(2 * side - 1, 0, 0),
            )
            copy.start()
            moved_x[order, e] = copy
    middle_grad = dot(onehot_t[...], here_g)
    plane_sum = {e: middle_grad[PLANE * e : PLANE * (e + 1)] for e in range(3)}

    high, low = split_bf16(hidden * readout)
    atom_terms = dot(members, high) + dot(members, low)
    energy = dot(jnp.ones((8, WIDTH), F32), atom_terms, NT, HIGH)

    moved_yz = {}
    for e in (0, 2, 1):
        moved_x[0, e].wait_recv()
        moved_x[1, e].wait_recv()
        plane_sum[e] = plane_sum[e] + grad_recv[0, e].astype(F32) + grad_recv[1, e].astype(F32)
        plane_send[e] = plane_sum[e].astype(BF16)
        for k, (dy, dz) in enumerate(PARTNERS):
            if dy == e - 1:
                rows_send = pl.ds(*ROWS[dz])
                copy = remote(
                    plane_send.at[e, rows_send],
                    plane_recv.at[k, pl.ds(0, ROWS[dz][1])],
                    send_c.at[16 + k],
                    recv_c.at[16 + k],
                    device(0, dy, dz),
                )
                copy.start()
                moved_yz[k] = copy
    for copy in moved_yz.values():
        copy.wait_recv()
    sends.extend(moved_x.values())
    sends.extend(moved_yz.values())
    parts = {0: plane_sum[1][0:128]}
    for k, (dy, dz) in enumerate(PARTNERS):
        got = plane_recv[k, 0 : ROWS[dz][1], :].astype(F32)
        parts[dz] = got if dz not in parts else parts[dz] + got
    owned = parts[0] + jnp.concatenate([parts[1], parts[-1]], axis=0)

    owned_edges = jnp.broadcast_to((owned * (1.0 / NEIGH))[:, None, :], (ATOMS, NEIGH, WIDTH)).reshape(EDGES, WIDTH)
    summed_g = (edge_buf[...] + owned_edges) * upd_d[...]
    edge_buf[...] = summed_g
    summed_b[...] = summed_g.astype(BF16)
    for j in range(GROUPS):
        span = slice(128 * j, 128 * (j + 1))
        placed(values, j, dot(diag_a[j], summed_b[span, :]).astype(BF16))
    for value, weight in zip(values, update_w):
        value[...] = (dot(value[...], weight, NT) * (1.0 / NEIGH)).astype(BF16)
    angular_g = [[] for _ in range(9)]
    for j in range(GROUPS):
        span = slice(128 * j, 128 * (j + 1))
        value_g = gathered(values, j)
        latent_buf[span, :] = dot(diag_at[j], value_g)
        all_g = dot(
            jnp.concatenate([gathered(mixes, j), value_g], axis=1),
            jnp.concatenate([summed_b[span, :], env_buf[span, :]], axis=1),
            NT,
        )
        for m in range(1, 9):
            angular_g[m].append(
                jnp.sum(all_g[GROUP * m : GROUP * (m + 1)] * group_mask, axis=0, keepdims=True)
            )
    latent_g = dot(latent_buf[...].astype(BF16), env_ref[...], NT).astype(BF16).astype(F32)
    mixed_g = ((edge_buf[...] + latent_g) * mix_d[...]).astype(BF16)
    act_g = dot(mixed_g, mix_ref[...], NT).astype(BF16).astype(F32)
    before_g = (act_g * act_d[...]).astype(BF16)
    basis_g = dot(radial_ref[...], before_g, NT).astype(BF16).astype(F32)

    distance_g = jnp.sum(basis_g * basis_d, axis=0, keepdims=True)
    g = [jnp.concatenate(parts_m, axis=1) if parts_m else None for parts_m in angular_g]
    gu_x = g[1] + ROOT3 * (u_y * g[4] + u_z * g[7] + u_x * g[8])
    gu_y = g[2] + ROOT3 * (u_x * g[4] + u_z * g[5] - u_y * g[8])
    gu_z = g[3] + ROOT3 * (u_y * g[5] + u_x * g[7]) + 3.0 * u_z * g[6]
    along = distance_g - inverse * (u_x * gu_x + u_y * gu_y + u_z * gu_z)
    pull = [-(gu * inverse + u * along) for gu, u in ((gu_x, u_x), (gu_y, u_y), (gu_z, u_z))]
    pull4 = jnp.concatenate(pull + [jnp.zeros_like(u_x)], axis=0)
    high = pull4.astype(BF16).astype(F32)
    pull8 = jnp.concatenate([high, pull4 - high], axis=0)

    pulls = jnp.concatenate([jnp.where(level == a, pull8, 0.0) for a in range(3)], axis=0).astype(BF16)
    spread_f = dot(pulls, onehot_t[...], NT)
    for a in range(3):
        level_f = spread_f[8 * a : 8 * a + 4] + spread_f[8 * a + 4 : 8 * a + 8]
        for i in range(6):
            force_tab[3 * a + i // 2, i % 2] = level_f[:, 128 * i : 128 * (i + 1)]
    moved_f = []
    for k, (dx, dy, dz) in enumerate(AROUND):
        copy = remote(
            force_tab.at[3 * dx + dy + 4, 1 if dz else 0],
            force_recv.at[k],
            send_f.at[k],
            recv_f.at[k],
            device(dx, dy, dz),
        )
        copy.start()
        moved_f.append(copy)
    both = dot(pull8.astype(BF16), members, NT)
    own_f = both[0:4] + both[4:8]
    for copy in moved_f:
        copy.wait_recv()
    sends.extend(moved_f)
    total = force_tab[4, 0] - own_f
    ends = {}
    for k, (dx, dy, dz) in enumerate(AROUND):
        got = force_recv[k]
        if dz == 0:
            total = total + got
        else:
            ends[dz] = got if dz not in ends else ends[dz] + got
    total = total + jnp.where(half_lane, ends[1], ends[-1])
    shown = [energy[0:1]] + [total[c : c + 1] for c in range(3)]
    out_ref[0, 0] = jnp.concatenate(
        [
            jnp.concatenate([row[:, SLOTS * z : SLOTS * (z + 1)] for row in shown], axis=1)
            for z in range(CELLS_Z)
        ],
        axis=0,
    )
    for copy in sends:
        copy.wait_send()


def on_device(
    positions,
    species,
    neighbors,
    center_table,
    neighbor_table,
    radial_weight,
    mix_weight,
    env_weight,
    update_weight,
    second_weight,
    readout,
):
    dma = pltpu.SemaphoreType.DMA
    vmem = pltpu.VMEM
    cells = positions.shape[:3]
    args = (
        positions,
        species,
        neighbors,
        center_table,
        neighbor_table,
        radial_weight,
        mix_weight,
        env_weight,
        update_weight,
        second_weight,
        readout.reshape(1, WIDTH),
    )
    both = pl.pallas_call(
        kernel,
        out_shape=jax.ShapeDtypeStruct((*cells, 4 * SLOTS), F32),
        in_specs=[pl.BlockSpec(memory_space=pl.ANY)] * len(args),
        out_specs=pl.BlockSpec(memory_space=pltpu.VMEM),
        scratch_shapes=[
            *(vmem(arg.shape, arg.dtype) for arg in args),
            dma((len(args),)),
            vmem((9, 3, 4, 128), F32),
            vmem((EDGES, LEVEL), BF16),
            vmem((LEVEL, EDGES), BF16),
            vmem((GROUPS, 128, 128), F32),
            vmem((EDGES, 128), F32),
            vmem((9, PLANE, WIDTH), BF16),
            vmem((24, WIDTH), F32),
            vmem((EDGES, WIDTH), F32),
            vmem((EDGES, WIDTH), F32),
            vmem((EDGES, WIDTH), F32),
            vmem((EDGES, WIDTH), BF16),
            vmem((GROUPS, 9 * GROUP, 128), BF16),
            vmem((GROUPS, 128, 9 * GROUP), BF16),
            vmem((1 * ATOMS, WIDTH), BF16),
            vmem((3 * ATOMS, WIDTH), BF16),
            vmem((5 * ATOMS, WIDTH), BF16),
            vmem((1 * ATOMS, WIDTH), BF16),
            vmem((3 * ATOMS, WIDTH), BF16),
            vmem((5 * ATOMS, WIDTH), BF16),
            vmem((EDGES, WIDTH), BF16),
            vmem((EDGES, WIDTH), F32),
            vmem((EDGES, WIDTH), F32),
            vmem((2, 3, PLANE, WIDTH), BF16),
            vmem((2, 3, PLANE, WIDTH), BF16),
            vmem((3, PLANE, WIDTH), BF16),
            vmem((8, 128, WIDTH), BF16),
            vmem((9, 2, 4, 128), F32),
            vmem((26, 4, 128), F32),
            dma((26,)),
            dma((26,)),
            dma((24,)),
            dma((24,)),
            dma((14,)),
            dma((14,)),
            dma((6,)),
            dma((6,)),
            dma((26,)),
            dma((26,)),
        ],
        compiler_params=pltpu.CompilerParams(collective_id=0, has_side_effects=True),
    )(*args)
    return both[..., :SLOTS], both[..., SLOTS:]


def solution(mesh):
    placed = (
        P("gx", "gy", "gz", None),
        P("gx", "gy", "gz", None),
        P("gx", "gy", "gz", None),
        P(),
        P(),
        P(),
        P(),
        P(),
        P(),
        P(),
        P(),
    )
    return jax.shard_map(
        on_device,
        mesh=mesh,
        in_specs=placed,
        out_specs=(P("gx", "gy", "gz", None), P("gx", "gy", "gz", None)),
        check_vma=False,
    )
```

time: 65.6 us -> 58.4 us (0.89)
  Pallas kernels: 63 us -> 55.7 us
    pallas_call x1, Pallas kernels: 63 us -> 55.7 us  [on_device(): pl.pallas_call(kernel, out_shape=jax.ShapeDtypeStruct((*cells, 4 * SLOTS)...]
    slice x0 -> x2, local copies, waits for them, and re-layouts: none -> 1.94 us  [on_device(): return (both[..., :SLOTS], both[..., SLOTS:])]
    unnamed x6 -> x2, local copies, waits for them, and re-layouts: 1.76 us -> 0.01 us
where the time goes in v2:
time: 58.4 us; the launch traced here: 58.3 us
  Pallas kernels  55.7 us (95%)
  local copies, waits for them, and re-layouts  1.94 us (3%)
  between operations  0.65 us (1%)
    pallas_call x1, Pallas kernels, on_device(): pl.pallas_call(kernel, out_shape=jax.ShapeDtypeStruct((*cells, 4 * SLOTS)...  55.7 us
    slice x2, local copies, waits for them, and re-layouts, on_device(): return (both[..., :SLOTS], both[..., SLOTS:])  1.94 us

profile of v2, /device:TPU:1, one launch (start us, length us, event | category | flops | bytes accessed | tf_op | source)
XLA Modules:
  0.0 58.3 jit_solution(1628651316190039417)
XLA Ops:
  0.6 55.7 %shard_map.122 = f32[1,1,2,256]{3,2,1,0:T(2,128)} custom-call(f32[1,1,2,192]{3,2,1,0:T(2,128)} %pos_in.1, s32[1,1,2,64]{3,2,1,0:T(2,128)} %spec_in.1, s32[1,1,2,512]{3,2,1,0:T(2,128)} %nbr_in.1, bf16[5,128]{1,0:T(8,128)(2,1)} %center_in.1, bf16[5,128]{1,0:T(8,128)(2,1)} %neighbor_in.1, bf16[8,128]{1,0:T(8,128)(2,1)} %radial_in.1, bf16[128,128]{1,0:T(8,128)(2,1)} %mix_in.1, ...), custom_call_target="tpu_custom_call" | custom-call | tf_op jit(solution)/shard_map/pallas_call | solution.py:593
  56.3 0.0 copy-start
  56.3 1.3 %slice.6 = f32[1,1,2,64]{3,2,1,0:T(2,128)} slice(f32[1,1,2,256]{3,2,1,0:T(2,128)} %shard_map.122), slice={[0:1], [0:1], [0:2], [0:64]} | slice | bytes 1024 | tf_op jit(solution)/shard_map/slice | solution.py:642
  57.6 0.0 copy-done
  57.6 0.7 %slice.7 = f32[1,1,2,192]{3,2,1,0:T(2,128)} slice(f32[1,1,2,256]{3,2,1,0:T(2,128)S(1)} %copy-done), slice={[0:1], [0:1], [0:2], [64:256]} | slice | bytes 3072 | tf_op jit(solution)/shard_map/slice | solution.py:642
Async XLA Ops:
  56.3 1.3 %copy-start = (f32[1,1,2,256]{3,2,1,0:T(2,128)S(1)}, f32[1,1,2,256]{3,2,1,0:T(2,128)}, u32[]{:S(2)}) copy-start(f32[1,1,2,256]{3,2,1,0:T(2,128)} %shard_map.122) | copy-start | bytes 6148

commit v3 on v2

--- a/solution.py
+++ b/solution.py
@@ -27,14 +27,14 @@
 GROUP = 16
 GROUPS = ATOMS // GROUP
 ROOT3 = math.sqrt(3.0)
+GRAD_CHUNKS = {0: ((0, PLANE),), 1: ((128, 128), (0, 128)), 2: ((0, PLANE),)}
 
 PARTNERS = ((1, -1), (-1, 1), (1, 1), (-1, -1), (0, 1), (0, -1), (1, 0), (-1, 0))
 AROUND = sorted(
     (d for d in itertools.product((-1, 0, 1), repeat=3) if any(d)), key=lambda d: -sum(abs(c) for c in d)
 )
-PART = {0: 0, 1: 1, -1: 2}
 ROWS = {0: (0, 128), 1: (128, 64), -1: (192, 64)}
-OWN_ROWS = {0: (0, 128), 1: (0, 64), -1: (64, 64)}
+SLOTS_YZ = tuple((64 * k, 64) if dz else (384 + 128 * (k - 6), 128) for k, (dy, dz) in enumerate(PARTNERS))
 
 
 def split_bf16(value):
@@ -110,22 +110,23 @@
     recv_a,
     send_c,
     recv_c,
-    send_x,
     recv_x,
-    send_d,
     recv_d,
-    send_f,
-    recv_f,
 ):
     size_x, size_y, size_z = lax.axis_size("gx"), lax.axis_size("gy"), lax.axis_size("gz")
     my_x, my_y, my_z = lax.axis_index("gx"), lax.axis_index("gy"), lax.axis_index("gz")
 
+    near = []
+    for index, size in ((my_x, size_x), (my_y, size_y), (my_z, size_z)):
+        near.append(
+            (index, jnp.where(index == size - 1, 0, index + 1), jnp.where(index == 0, size - 1, index - 1))
+        )
+
     def device(dx, dy, dz):
-        return (
-            lax.rem(my_x + (dx + size_x), size_x),
-            lax.rem(my_y + (dy + size_y), size_y),
-            lax.rem(my_z + (dz + size_z), size_z),
-        )
+        return near[0][dx], near[1][dy], near[2][dz]
+
+    def settle(ref, sem):
+        pltpu.make_async_copy(ref, ref, sem).wait()
 
     def remote(src, dst, send, recv, target):
         return pltpu.make_async_remote_copy(
@@ -157,14 +158,15 @@
     ]
     rows.append(jnp.concatenate([kinds[z : z + 1, :] for z in range(CELLS_Z)], axis=1))
     own_tile = jnp.concatenate(rows, axis=0)
-    tiles[4, 0] = own_tile
+    tiles[13] = own_tile
 
     pl.semaphore_wait(barrier, len(AROUND))
-
-    sends = []
 
     far_side = lax.rem(my_x, 2)
     sides = (far_side, 1 - far_side)
+
+    def x_device(side):
+        return jnp.where(side == 0, near[0][-1], near[0][1]), my_y, my_z
 
     def forward(source, dest, send, recv, k):
         copies = []
@@ -172,23 +174,22 @@
             copy = remote(
                 source,
                 dest(3 * (2 * side)),
-                send.at[2 * k + side],
+                send.at[1],
                 recv.at[2 * k + side],
-                device(1 - 2 * side, 0, 0),
+                x_device(1 - side),
             )
             copy.start()
             copies.append(copy)
-        sends.extend(copies)
         return copies
 
-    moved_a = []
-    for k, (dx, dy, dz) in enumerate(AROUND):
+    def tile_of(dx, dy, dz):
+        return 9 * (dx + 1) + 3 * (dy + 1) + (dz + 1)
+
+    for dx, dy, dz in AROUND:
         copy = remote(
-            tiles.at[4, 0], tiles.at[3 * dx + dy + 4, PART[dz]], send_a.at[k], recv_a.at[k], device(-dx, -dy, -dz)
+            tiles.at[13], tiles.at[tile_of(dx, dy, dz)], send_a.at[0], recv_a.at[0], device(-dx, -dy, -dz)
         )
         copy.start()
-        moved_a.append(copy)
-    sends.extend(moved_a)
 
     loads[2].wait()
     codes = nbr_ref[0, 0]
@@ -217,14 +218,14 @@
     weights[16 : 16 + spec_count, :] = neighbor_ref[...].astype(F32)
     before_w = weights[...].astype(BF16)
 
-    for copy in moved_a:
-        copy.wait_recv()
+    settle(tiles.at[pl.ds(0, len(AROUND))], recv_a.at[0])
+    settle(tiles.at[pl.ds(0, len(AROUND))], send_a.at[0])
 
     half_lane = lax.broadcasted_iota(jnp.int32, (4, 128), 1) < SLOTS
     halves = []
     for p in range(9):
-        halves.append(tiles[p, 0])
-        halves.append(jnp.where(half_lane, tiles[p, 1], tiles[p, 2]))
+        halves.append(tiles[3 * p + 1])
+        halves.append(jnp.where(half_lane, tiles[3 * p + 2], tiles[3 * p]))
     packed = [jnp.concatenate([halves[t], halves[t + 9]], axis=0) for t in range(9)]
     own8 = jnp.concatenate([own_tile, own_tile], axis=0)
     lane8 = lax.broadcasted_iota(jnp.int32, (8, 128), 1)
@@ -319,7 +320,7 @@
             span = slice(128 * j, 128 * (j + 1))
             spread_y = jnp.concatenate([angular[m][:, span] * group_mask for m in range(9)], axis=0)
             diag_a[j] = spread_y.astype(BF16)
-            diag_at[j] = jnp.transpose(spread_y).astype(BF16)
+            diag_at[j] = jnp.transpose(diag_a[j])
             placed(values, j, (dot(diag_a[j], env_buf[span, :]) * (1.0 / NEIGH)).astype(BF16))
         for value, mixed_l, weight, (start, stop) in zip(values, mixes, update_w, levels):
             rows_l = GROUP * (stop - start) * half_groups
@@ -344,7 +345,7 @@
             copy = remote(
                 table.at[4, own_rows],
                 table.at[4 + dy, rows_there],
-                send_c.at[k + 8 * z],
+                send_c.at[0],
                 recv_c.at[k + 8 * z],
                 device(0, -dy, -dz),
             )
@@ -352,10 +353,9 @@
             yz[dy, dz, z] = copy
         moved_c.append(
             forward(
-                table.at[4, own_rows], lambda a, own_rows=own_rows: table.at[a + 1, own_rows], send_x, recv_x, z
+                table.at[4, own_rows], lambda a, own_rows=own_rows: table.at[a + 1, own_rows], send_c, recv_x, z
             )
         )
-    sends.extend(yz.values())
 
     row_kinds = [target[:, 128 * j : 128 * (j + 1)].astype(F32) for j in range(8)]
     row_kinds += [level[:, 128 * j : 128 * (j + 1)].astype(F32) for j in range(8)]
@@ -388,15 +388,15 @@
     pair = pl.ds(0, 128)
     yz[0, 1, 0].wait_recv()
     yz[0, -1, 1].wait_recv()
-    moved_c.append(forward(table.at[4, ends], lambda a: table.at[a + 1, ends], send_x, recv_x, 2))
+    moved_c.append(forward(table.at[4, ends], lambda a: table.at[a + 1, ends], send_c, recv_x, 2))
     for k, dy in ((3, 1), (5, -1)):
         yz[dy, 0, 0].wait_recv()
         yz[dy, 0, 1].wait_recv()
-        moved_c.append(forward(table.at[4 + dy, pair], lambda a, dy=dy: table.at[a + 1 + dy, pair], send_x, recv_x, k))
+        moved_c.append(forward(table.at[4 + dy, pair], lambda a, dy=dy: table.at[a + 1 + dy, pair], send_c, recv_x, k))
         yz[dy, 1, 0].wait_recv()
         yz[dy, -1, 1].wait_recv()
         moved_c.append(
-            forward(table.at[4 + dy, ends], lambda a, dy=dy: table.at[a + 1 + dy, ends], send_x, recv_x, k + 1)
+            forward(table.at[4 + dy, ends], lambda a, dy=dy: table.at[a + 1 + dy, ends], send_c, recv_x, k + 1)
         )
     here = dot(onehot[...], jnp.concatenate([table[3], table[4], table[5]], axis=0))
     beside = jnp.zeros((EDGES, 2 * WIDTH), F32)
@@ -433,16 +433,18 @@
         grads = dot(onehot_t[PLANE * e : PLANE * (e + 1), :], beside_g).astype(BF16)
         grad_send[0, e] = grads[:, 0:WIDTH]
         grad_send[1, e] = grads[:, WIDTH : 2 * WIDTH]
-        for order, side in enumerate(sides):
-            copy = remote(
-                grad_send.at[side, e],
-                grad_recv.at[side, e],
-                send_d.at[3 * side + e],
-                recv_d.at[3 * side + e],
-                device(2 * side - 1, 0, 0),
-            )
-            copy.start()
-            moved_x[order, e] = copy
+        for c, (first, count) in enumerate(GRAD_CHUNKS[e]):
+            chunk = pl.ds(first, count)
+            for order, side in enumerate(sides):
+                copy = remote(
+                    grad_send.at[side, e, chunk],
+                    grad_recv.at[side, e, chunk],
+                    send_c.at[2],
+                    recv_d.at[4 * side + e + 2 * c],
+                    x_device(side),
+                )
+                copy.start()
+                moved_x[order, e, c] = copy
     middle_grad = dot(onehot_t[...], here_g)
     plane_sum = {e: middle_grad[PLANE * e : PLANE * (e + 1)] for e in range(3)}
 
@@ -450,31 +452,38 @@
     atom_terms = dot(members, high) + dot(members, low)
     energy = dot(jnp.ones((8, WIDTH), F32), atom_terms, NT, HIGH)
 
-    moved_yz = {}
     for e in (0, 2, 1):
-        moved_x[0, e].wait_recv()
-        moved_x[1, e].wait_recv()
-        plane_sum[e] = plane_sum[e] + grad_recv[0, e].astype(F32) + grad_recv[1, e].astype(F32)
-        plane_send[e] = plane_sum[e].astype(BF16)
+        moved_x[0, e, 0].wait_recv()
+        moved_x[1, e, 0].wait_recv()
+        if e == 1:
+            arrived = slice(128, 256)
+        else:
+            arrived = slice(0, 256)
+        plane_send[e, arrived, :] = (
+            plane_sum[e][arrived] + grad_recv[0, e, arrived, :].astype(F32) + grad_recv[1, e, arrived, :].astype(F32)
+        ).astype(BF16)
         for k, (dy, dz) in enumerate(PARTNERS):
             if dy == e - 1:
-                rows_send = pl.ds(*ROWS[dz])
                 copy = remote(
-                    plane_send.at[e, rows_send],
-                    plane_recv.at[k, pl.ds(0, ROWS[dz][1])],
-                    send_c.at[16 + k],
-                    recv_c.at[16 + k],
+                    plane_send.at[e, pl.ds(*ROWS[dz])],
+                    plane_recv.at[pl.ds(*SLOTS_YZ[k])],
+                    send_c.at[3],
+                    recv_c.at[16],
                     device(0, dy, dz),
                 )
                 copy.start()
-                moved_yz[k] = copy
-    for copy in moved_yz.values():
-        copy.wait_recv()
-    sends.extend(moved_x.values())
-    sends.extend(moved_yz.values())
-    parts = {0: plane_sum[1][0:128]}
+    moved_x[0, 1, 1].wait_recv()
+    moved_x[1, 1, 1].wait_recv()
+    own_sum = plane_sum[1][0:128] + grad_recv[0, 1, 0:128, :].astype(F32) + grad_recv[1, 1, 0:128, :].astype(F32)
+    settle(plane_recv, send_c.at[0])
+    settle(table.at[pl.ds(0, 6)], send_c.at[1])
+    settle(grad_send, send_c.at[2])
+    settle(plane_recv, send_c.at[3])
+    settle(plane_recv, recv_c.at[16])
+    parts = {0: own_sum}
     for k, (dy, dz) in enumerate(PARTNERS):
-        got = plane_recv[k, 0 : ROWS[dz][1], :].astype(F32)
+        first, count = SLOTS_YZ[k]
+        got = plane_recv[first : first + count, :].astype(F32)
         parts[dz] = got if dz not in parts else parts[dz] + got
     owned = parts[0] + jnp.concatenate([parts[1], parts[-1]], axis=0)
 
@@ -524,22 +533,18 @@
         level_f = spread_f[8 * a : 8 * a + 4] + spread_f[8 * a + 4 : 8 * a + 8]
         for i in range(6):
             force_tab[3 * a + i // 2, i % 2] = level_f[:, 128 * i : 128 * (i + 1)]
-    moved_f = []
     for k, (dx, dy, dz) in enumerate(AROUND):
         copy = remote(
             force_tab.at[3 * dx + dy + 4, 1 if dz else 0],
             force_recv.at[k],
-            send_f.at[k],
-            recv_f.at[k],
+            send_a.at[1],
+            recv_a.at[1],
             device(dx, dy, dz),
         )
         copy.start()
-        moved_f.append(copy)
     both = dot(pull8.astype(BF16), members, NT)
     own_f = both[0:4] + both[4:8]
-    for copy in moved_f:
-        copy.wait_recv()
-    sends.extend(moved_f)
+    settle(force_recv, recv_a.at[1])
     total = force_tab[4, 0] - own_f
     ends = {}
     for k, (dx, dy, dz) in enumerate(AROUND):
@@ -557,8 +562,7 @@
         ],
         axis=0,
     )
-    for copy in sends:
-        copy.wait_send()
+    settle(force_recv, send_a.at[1])
 
 
 def on_device(
@@ -598,7 +602,7 @@
         scratch_shapes=[
             *(vmem(arg.shape, arg.dtype) for arg in args),
             dma((len(args),)),
-            vmem((9, 3, 4, 128), F32),
+            vmem((27, 4, 128), F32),
             vmem((EDGES, LEVEL), BF16),
             vmem((LEVEL, EDGES), BF16),
             vmem((GROUPS, 128, 128), F32),
@@ -623,19 +627,15 @@
             vmem((2, 3, PLANE, WIDTH), BF16),
             vmem((2, 3, PLANE, WIDTH), BF16),
             vmem((3, PLANE, WIDTH), BF16),
-            vmem((8, 128, WIDTH), BF16),
+            vmem((640, WIDTH), BF16),
             vmem((9, 2, 4, 128), F32),
             vmem((26, 4, 128), F32),
-            dma((26,)),
-            dma((26,)),
-            dma((24,)),
-            dma((24,)),
+            dma((2,)),
+            dma((2,)),
+            dma((4,)),
+            dma((17,)),
             dma((14,)),
-            dma((14,)),
-            dma((6,)),
-            dma((6,)),
-            dma((26,)),
-            dma((26,)),
+            dma((8,)),
         ],
         compiler_params=pltpu.CompilerParams(collective_id=0, has_side_effects=True),
     )(*args)

time: 58.4 us -> 56.8 us (0.973)
  Pallas kernels: 55.7 us -> 54.1 us
    pallas_call x1, Pallas kernels: 55.7 us -> 54.1 us  [on_device(): pl.pallas_call(kernel, out_shape=jax.ShapeDtypeStruct((*cells, 4 * SLOTS)...]
where the time goes in v3:
time: 56.8 us; the launch traced here: 56.7 us
  Pallas kernels  54.1 us (95%)
  local copies, waits for them, and re-layouts  1.94 us (3%)
  between operations  0.65 us (1%)
    pallas_call x1, Pallas kernels, on_device(): pl.pallas_call(kernel, out_shape=jax.ShapeDtypeStruct((*cells, 4 * SLOTS)...  54.1 us
    slice x2, local copies, waits for them, and re-layouts, on_device(): return (both[..., :SLOTS], both[..., SLOTS:])  1.94 us

profile of v3, /device:TPU:1, one launch (start us, length us, event | category | flops | bytes accessed | tf_op | source)
XLA Modules:
  0.0 56.7 jit_solution(13381856110205001125)
XLA Ops:
  0.6 54.1 %shard_map.122 = f32[1,1,2,256]{3,2,1,0:T(2,128)} custom-call(f32[1,1,2,192]{3,2,1,0:T(2,128)} %pos_in.1, s32[1,1,2,64]{3,2,1,0:T(2,128)} %spec_in.1, s32[1,1,2,512]{3,2,1,0:T(2,128)} %nbr_in.1, bf16[5,128]{1,0:T(8,128)(2,1)} %center_in.1, bf16[5,128]{1,0:T(8,128)(2,1)} %neighbor_in.1, bf16[8,128]{1,0:T(8,128)(2,1)} %radial_in.1, bf16[128,128]{1,0:T(8,128)(2,1)} %mix_in.1, ...), custom_call_target="tpu_custom_call" | custom-call | tf_op jit(solution)/shard_map/pallas_call | solution.py:597
  54.7 0.0 copy-start
  54.7 1.3 %slice.6 = f32[1,1,2,64]{3,2,1,0:T(2,128)} slice(f32[1,1,2,256]{3,2,1,0:T(2,128)} %shard_map.122), slice={[0:1], [0:1], [0:2], [0:64]} | slice | bytes 1024 | tf_op jit(solution)/shard_map/slice | solution.py:642
  56.0 0.0 copy-done
  56.0 0.7 %slice.7 = f32[1,1,2,192]{3,2,1,0:T(2,128)} slice(f32[1,1,2,256]{3,2,1,0:T(2,128)S(1)} %copy-done), slice={[0:1], [0:1], [0:2], [64:256]} | slice | bytes 3072 | tf_op jit(solution)/shard_map/slice | solution.py:642
Async XLA Ops:
  54.7 1.3 %copy-start = (f32[1,1,2,256]{3,2,1,0:T(2,128)S(1)}, f32[1,1,2,256]{3,2,1,0:T(2,128)}, u32[]{:S(2)}) copy-start(f32[1,1,2,256]{3,2,1,0:T(2,128)} %shard_map.122) | copy-start | bytes 6148

commit v4 on v3

--- a/solution.py
+++ b/solution.py
@@ -65,7 +65,8 @@
     update_in,
     second_in,
     readout_in,
-    out_ref,
+    energy_ref,
+    force_ref,
     pos_ref,
     spec_ref,
     nbr_ref,
@@ -83,6 +84,7 @@
     onehot_t,
     target_col,
     level_col,
+    level_mask,
     table,
     weights,
     act_d,
@@ -209,6 +211,36 @@
     level = flat(step_a)
     offsets = [flat(step - 1).astype(F32) for step in (step_a, step_e, row_z)]
 
+    row_kinds = [target[:, 128 * j : 128 * (j + 1)].astype(F32) for j in range(8)]
+    row_kinds += [level[:, 128 * j : 128 * (j + 1)].astype(F32) for j in range(8)]
+    columns = jnp.transpose(jnp.concatenate(row_kinds + [jnp.zeros((112, 128), F32)], axis=0))
+    for j in range(8):
+        target_col[j] = jnp.broadcast_to(columns[:, j : j + 1], (128, 128))
+        level_col[128 * j : 128 * (j + 1), :] = jnp.broadcast_to(columns[:, 8 + j : 9 + j], (128, 128))
+
+    def build(j, carry):
+        first = pl.multiple_of(j * 128, 128)
+        level_j = level_col[pl.ds(first, 128), :]
+        for a in range(3):
+            level_mask[a, pl.ds(first, 128), :] = (level_j == float(a)).astype(F32).astype(BF16)
+        lane = lax.broadcasted_iota(jnp.int32, (128, 128), 1).astype(F32)
+        column = target_col[j]
+        for t in range(LEVEL // 128):
+            onehot[pl.ds(first, 128), 128 * t : 128 * (t + 1)] = (
+                (column == lane + float(128 * t)).astype(F32).astype(BF16)
+            )
+        return carry
+
+    lax.fori_loop(0, GROUPS, build, 0)
+
+    def build_t(t, carry):
+        first = pl.multiple_of(t * 128, 128)
+        row = lax.broadcasted_iota(jnp.int32, (128, EDGES), 0) + first
+        onehot_t[pl.ds(first, 128), :] = (row == target).astype(F32).astype(BF16)
+        return carry
+
+    lax.fori_loop(0, LEVEL // 128, build_t, 0)
+
     for load in loads[3:]:
         load.wait()
     weights[...] = jnp.zeros_like(weights)
@@ -357,33 +389,6 @@
             )
         )
 
-    row_kinds = [target[:, 128 * j : 128 * (j + 1)].astype(F32) for j in range(8)]
-    row_kinds += [level[:, 128 * j : 128 * (j + 1)].astype(F32) for j in range(8)]
-    columns = jnp.transpose(jnp.concatenate(row_kinds + [jnp.zeros((112, 128), F32)], axis=0))
-    for j in range(8):
-        target_col[j] = jnp.broadcast_to(columns[:, j : j + 1], (128, 128))
-        level_col[128 * j : 128 * (j + 1), :] = jnp.broadcast_to(columns[:, 8 + j : 9 + j], (128, 128))
-
-    def build(j, carry):
-        first = pl.multiple_of(j * 128, 128)
-        lane = lax.broadcasted_iota(jnp.int32, (128, 128), 1).astype(F32)
-        column = target_col[j]
-        for t in range(LEVEL // 128):
-            onehot[pl.ds(first, 128), 128 * t : 128 * (t + 1)] = (
-                (column == lane + float(128 * t)).astype(F32).astype(BF16)
-            )
-        return carry
-
-    lax.fori_loop(0, GROUPS, build, 0)
-
-    def build_t(t, carry):
-        first = pl.multiple_of(t * 128, 128)
-        row = lax.broadcasted_iota(jnp.int32, (128, EDGES), 0) + first
-        onehot_t[pl.ds(first, 128), :] = (row == target).astype(F32).astype(BF16)
-        return carry
-
-    lax.fori_loop(0, LEVEL // 128, build_t, 0)
-
     ends = pl.ds(128, 128)
     pair = pl.ds(0, 128)
     yz[0, 1, 0].wait_recv()
@@ -420,12 +425,9 @@
     hidden = hidden_in * gate
     hidden_g = (readout * (gate + hidden * (1.0 - gate))).astype(BF16)
     product_g = dot(hidden_g, second_w, NT).astype(BF16).astype(F32)
-    other_g = product_g * edge
-    none = jnp.zeros_like(other_g)
-    beside_g = jnp.concatenate(
-        [jnp.where(levels_e == 0.0, other_g, none), jnp.where(levels_e == 2.0, other_g, none)], axis=1
-    ).astype(BF16)
-    here_g = jnp.where(levels_e == 1.0, other_g, none).astype(BF16)
+    other_g = (product_g * edge).astype(BF16)
+    beside_g = jnp.concatenate([other_g * level_mask[0], other_g * level_mask[2]], axis=1)
+    here_g = other_g * level_mask[1]
     edge_buf[...] = product_g * other_latent
 
     moved_x = {}
@@ -554,10 +556,12 @@
         else:
             ends[dz] = got if dz not in ends else ends[dz] + got
     total = total + jnp.where(half_lane, ends[1], ends[-1])
-    shown = [energy[0:1]] + [total[c : c + 1] for c in range(3)]
-    out_ref[0, 0] = jnp.concatenate(
+    energy_ref[0, 0] = jnp.concatenate(
+        [energy[0:1, SLOTS * z : SLOTS * (z + 1)] for z in range(CELLS_Z)], axis=0
+    )
+    force_ref[0, 0] = jnp.concatenate(
         [
-            jnp.concatenate([row[:, SLOTS * z : SLOTS * (z + 1)] for row in shown], axis=1)
+            jnp.concatenate([total[c : c + 1, SLOTS * z : SLOTS * (z + 1)] for c in range(3)], axis=1)
             for z in range(CELLS_Z)
         ],
         axis=0,
@@ -594,11 +598,11 @@
         second_weight,
         readout.reshape(1, WIDTH),
     )
-    both = pl.pallas_call(
+    energies, forces = pl.pallas_call(
         kernel,
-        out_shape=jax.ShapeDtypeStruct((*cells, 4 * SLOTS), F32),
+        out_shape=(pltpu.VMEM((*cells, SLOTS), F32), pltpu.VMEM((*cells, 3 * SLOTS), F32)),
         in_specs=[pl.BlockSpec(memory_space=pl.ANY)] * len(args),
-        out_specs=pl.BlockSpec(memory_space=pltpu.VMEM),
+        out_specs=[pl.BlockSpec(memory_space=pltpu.VMEM)] * 2,
         scratch_shapes=[
             *(vmem(arg.shape, arg.dtype) for arg in args),
             dma((len(args),)),
@@ -607,6 +611,7 @@
             vmem((LEVEL, EDGES), BF16),
             vmem((GROUPS, 128, 128), F32),
             vmem((EDGES, 128), F32),
+            vmem((3, EDGES, 128), BF16),
             vmem((9, PLANE, WIDTH), BF16),
             vmem((24, WIDTH), F32),
             vmem((EDGES, WIDTH), F32),
@@ -639,7 +644,7 @@
         ],
         compiler_params=pltpu.CompilerParams(collective_id=0, has_side_effects=True),
     )(*args)
-    return both[..., :SLOTS], both[..., SLOTS:]
+    return energies, forces
 
 
 def solution(mesh):

time: 56.8 us -> 55.3 us (0.974)
  local copies, waits for them, and re-layouts: 1.94 us -> 1.14 us
  Pallas kernels: 54.1 us -> 53.4 us
    slice x2 -> x0, local copies, waits for them, and re-layouts: 1.94 us -> none  [on_device(): return (both[..., :SLOTS], both[..., SLOTS:])]
    unnamed x2, local copies, waits for them, and re-layouts: 0.01 us -> 1.14 us
    pallas_call x1, Pallas kernels: 54.1 us -> 53.4 us  [on_device(): pl.pallas_call(kernel, out_shape=(pltpu.VMEM((*cells, SLOTS), F32), pltpu...]
where the time goes in v4:
time: 55.3 us; the launch traced here: 55.2 us
  Pallas kernels  53.4 us (97%)
  local copies, waits for them, and re-layouts  1.14 us (2%)
  between operations  0.64 us (1%)
    pallas_call x1, Pallas kernels, on_device(): pl.pallas_call(kernel, out_shape=(pltpu.VMEM((*cells, SLOTS), F32), pltpu...  53.4 us
    unnamed x2, local copies, waits for them, and re-layouts  1.14 us

profile of v4, /device:TPU:1, one launch (start us, length us, event | category | flops | bytes accessed | tf_op | source)
XLA Modules:
  0.0 55.2 jit_solution(2748500256464229302)
XLA Ops:
  0.6 53.4 %shard_map.122 = (f32[1,1,2,64]{3,2,1,0:T(2,128)S(1)}, f32[1,1,2,192]{3,2,1,0:T(2,128)S(1)}) custom-call(f32[1,1,2,192]{3,2,1,0:T(2,128)} %pos_in.1, s32[1,1,2,64]{3,2,1,0:T(2,128)} %spec_in.1, s32[1,1,2,512]{3,2,1,0:T(2,128)} %nbr_in.1, bf16[5,128]{1,0:T(8,128)(2,1)} %center_in.1, bf16[5,128]{1,0:T(8,128)(2,1)} %neighbor_in.1, bf16[8,128]{1,0:T(8,128)(2,1)} %radial_in.1, ...), custom_call_target="tpu_custom_call" | custom-call | tf_op jit(solution)/shard_map/pallas_call | solution.py:601
  54.0 0.6 %copy.15 = f32[1,1,2,64]{3,2,1,0:T(2,128)} copy(f32[1,1,2,64]{3,2,1,0:T(2,128)S(1)} %get-tuple-element.2) | data formatting | bytes 1024
  54.6 0.6 %copy.16 = f32[1,1,2,192]{3,2,1,0:T(2,128)} copy(f32[1,1,2,192]{3,2,1,0:T(2,128)S(1)} %get-tuple-element.3) | data formatting | bytes 3072

commit v5 on v4

--- a/solution.py
+++ b/solution.py
@@ -27,7 +27,9 @@
 GROUP = 16
 GROUPS = ATOMS // GROUP
 ROOT3 = math.sqrt(3.0)
-GRAD_CHUNKS = {0: ((0, PLANE),), 1: ((128, 128), (0, 128)), 2: ((0, PLANE),)}
+PIECE_ORDER = {0: 0, 1: 1, -1: 2}
+GRAD_ENDS, GRAD_OWN = (128, 128), (0, 128)
+GRAD_ORDER = ((0, ((0, 0),)), (2, ((2, 0), (0, 1), (2, 1))), (1, ((1, 0), (1, 1))))
 
 PARTNERS = ((1, -1), (-1, 1), (1, 1), (-1, -1), (0, 1), (0, -1), (1, 0), (-1, 0))
 AROUND = sorted(
@@ -135,19 +137,20 @@
             src_ref=src, dst_ref=dst, send_sem=send, recv_sem=recv, device_id=target, device_id_type=MESH
         )
 
+    sources = (
+        pos_in, spec_in, nbr_in, center_in, neighbor_in, radial_in, mix_in, env_in, update_in, second_in, readout_in
+    )
+    places = (
+        pos_ref, spec_ref, nbr_ref, center_ref, neighbor_ref, radial_ref, mix_ref, env_ref, update_ref, second_ref,
+        readout_ref,
+    )
+    loads = [pltpu.make_async_copy(src, dst, load_sem.at[k]) for k, (src, dst) in enumerate(zip(sources, places))]
+    for load in loads[:3]:
+        load.start()
     barrier = pltpu.get_barrier_semaphore()
     for step in AROUND:
         pl.semaphore_signal(barrier, inc=1, device_id=device(*step), device_id_type=MESH)
-
-    sources = (
-        pos_in, spec_in, nbr_in, center_in, neighbor_in, radial_in, mix_in, env_in, update_in, second_in, readout_in
-    )
-    places = (
-        pos_ref, spec_ref, nbr_ref, center_ref, neighbor_ref, radial_ref, mix_ref, env_ref, update_ref, second_ref,
-        readout_ref,
-    )
-    loads = [pltpu.make_async_copy(src, dst, load_sem.at[k]) for k, (src, dst) in enumerate(zip(sources, places))]
-    for load in loads:
+    for load in loads[3:]:
         load.start()
     loads[0].wait()
     loads[1].wait()
@@ -336,7 +339,7 @@
     half_edges = EDGES // CELLS_Z
     half_groups = GROUPS // CELLS_Z
     yz = {}
-    moved_c = []
+    moved_c = {0: [], 1: [], -1: []}
     for z in range(CELLS_Z):
         block = slice(half_edges * z, half_edges * (z + 1))
         before = dot(features[block, :], before_w)
@@ -383,32 +386,27 @@
             )
             copy.start()
             yz[dy, dz, z] = copy
-        moved_c.append(
-            forward(
-                table.at[4, own_rows], lambda a, own_rows=own_rows: table.at[a + 1, own_rows], send_c, recv_x, z
-            )
-        )
-
-    ends = pl.ds(128, 128)
-    pair = pl.ds(0, 128)
-    yz[0, 1, 0].wait_recv()
-    yz[0, -1, 1].wait_recv()
-    moved_c.append(forward(table.at[4, ends], lambda a: table.at[a + 1, ends], send_c, recv_x, 2))
-    for k, dy in ((3, 1), (5, -1)):
-        yz[dy, 0, 0].wait_recv()
-        yz[dy, 0, 1].wait_recv()
-        moved_c.append(forward(table.at[4 + dy, pair], lambda a, dy=dy: table.at[a + 1 + dy, pair], send_c, recv_x, k))
-        yz[dy, 1, 0].wait_recv()
-        yz[dy, -1, 1].wait_recv()
-        moved_c.append(
-            forward(table.at[4 + dy, ends], lambda a, dy=dy: table.at[a + 1 + dy, ends], send_c, recv_x, k + 1)
-        )
+        moved_c[0] += forward(
+            table.at[4, own_rows], lambda a, own_rows=own_rows: table.at[a + 1, own_rows], send_c, recv_x, z
+        )
+
+    k = CELLS_Z
+    for (dy, dz, z), copy in sorted(yz.items(), key=lambda item: (item[0][2], PIECE_ORDER[item[0][0]])):
+        copy.wait_recv()
+        rows_here = pl.ds(SLOTS * z, SLOTS) if dz == 0 else pl.ds(*ROWS[dz])
+        moved_c[dy] += forward(
+            table.at[4 + dy, rows_here],
+            lambda a, dy=dy, rows_here=rows_here: table.at[a + 1 + dy, rows_here],
+            send_c,
+            recv_x,
+            k,
+        )
+        k += 1
     here = dot(onehot[...], jnp.concatenate([table[3], table[4], table[5]], axis=0))
     beside = jnp.zeros((EDGES, 2 * WIDTH), F32)
-    for e, chunks in ((1, (0, 1, 2)), (2, (3, 4)), (0, (5, 6))):
-        for c in chunks:
-            for copy in moved_c[c]:
-                copy.wait_recv()
+    for e in (1, 2, 0):
+        for copy in moved_c[e - 1]:
+            copy.wait_recv()
         pair_e = jnp.concatenate([table[e], table[6 + e]], axis=1)
         beside = beside + dot(onehot[:, PLANE * e : PLANE * (e + 1)], pair_e)
     levels_e = level_col[...]
@@ -431,22 +429,22 @@
     edge_buf[...] = product_g * other_latent
 
     moved_x = {}
-    for e in (0, 2, 1):
+    for e, chunks in GRAD_ORDER:
         grads = dot(onehot_t[PLANE * e : PLANE * (e + 1), :], beside_g).astype(BF16)
         grad_send[0, e] = grads[:, 0:WIDTH]
         grad_send[1, e] = grads[:, WIDTH : 2 * WIDTH]
-        for c, (first, count) in enumerate(GRAD_CHUNKS[e]):
-            chunk = pl.ds(first, count)
+        for e_sent, c in chunks:
+            chunk = pl.ds(*(GRAD_OWN if c else GRAD_ENDS))
             for order, side in enumerate(sides):
                 copy = remote(
-                    grad_send.at[side, e, chunk],
-                    grad_recv.at[side, e, chunk],
+                    grad_send.at[side, e_sent, chunk],
+                    grad_recv.at[side, e_sent, chunk],
                     send_c.at[2],
-                    recv_d.at[4 * side + e + 2 * c],
+                    recv_d.at[6 * side + 2 * e_sent + c],
                     x_device(side),
                 )
                 copy.start()
-                moved_x[order, e, c] = copy
+                moved_x[order, e_sent, c] = copy
     middle_grad = dot(onehot_t[...], here_g)
     plane_sum = {e: middle_grad[PLANE * e : PLANE * (e + 1)] for e in range(3)}
 
@@ -454,18 +452,16 @@
     atom_terms = dot(members, high) + dot(members, low)
     energy = dot(jnp.ones((8, WIDTH), F32), atom_terms, NT, HIGH)
 
-    for e in (0, 2, 1):
-        moved_x[0, e, 0].wait_recv()
-        moved_x[1, e, 0].wait_recv()
-        if e == 1:
-            arrived = slice(128, 256)
-        else:
-            arrived = slice(0, 256)
+    for e, c in ((0, 0), (2, 0), (0, 1), (2, 1), (1, 0)):
+        moved_x[0, e, c].wait_recv()
+        moved_x[1, e, c].wait_recv()
+        first, count = GRAD_OWN if c else GRAD_ENDS
+        arrived = slice(first, first + count)
         plane_send[e, arrived, :] = (
             plane_sum[e][arrived] + grad_recv[0, e, arrived, :].astype(F32) + grad_recv[1, e, arrived, :].astype(F32)
         ).astype(BF16)
         for k, (dy, dz) in enumerate(PARTNERS):
-            if dy == e - 1:
+            if dy == e - 1 and (dz == 0) == (c == 1):
                 copy = remote(
                     plane_send.at[e, pl.ds(*ROWS[dz])],
                     plane_recv.at[pl.ds(*SLOTS_YZ[k])],
@@ -639,8 +635,8 @@
             dma((2,)),
             dma((4,)),
             dma((17,)),
-            dma((14,)),
-            dma((8,)),
+            dma((24,)),
+            dma((12,)),
         ],
         compiler_params=pltpu.CompilerParams(collective_id=0, has_side_effects=True),
     )(*args)

time: 55.3 us -> 55 us (level)
  no operation moved by 1% of the time
where the time goes in v5:
time: 55 us; the launch traced here: 54.8 us
  Pallas kernels  53 us (96%)
  local copies, waits for them, and re-layouts  1.14 us (2%)
  between operations  0.64 us (1%)
    pallas_call x1, Pallas kernels, on_device(): pl.pallas_call(kernel, out_shape=(pltpu.VMEM((*cells, SLOTS), F32), pltpu...  53 us
    unnamed x2, local copies, waits for them, and re-layouts  1.14 us

profile of v5, /device:TPU:1, one launch (start us, length us, event | category | flops | bytes accessed | tf_op | source)
XLA Modules:
  0.0 54.8 jit_solution(1041809167926979157)
XLA Ops:
  0.6 53.0 %shard_map.122 = (f32[1,1,2,64]{3,2,1,0:T(2,128)S(1)}, f32[1,1,2,192]{3,2,1,0:T(2,128)S(1)}) custom-call(f32[1,1,2,192]{3,2,1,0:T(2,128)} %pos_in.1, s32[1,1,2,64]{3,2,1,0:T(2,128)} %spec_in.1, s32[1,1,2,512]{3,2,1,0:T(2,128)} %nbr_in.1, bf16[5,128]{1,0:T(8,128)(2,1)} %center_in.1, bf16[5,128]{1,0:T(8,128)(2,1)} %neighbor_in.1, bf16[8,128]{1,0:T(8,128)(2,1)} %radial_in.1, ...), custom_call_target="tpu_custom_call" | custom-call | tf_op jit(solution)/shard_map/pallas_call | solution.py:597
  53.7 0.6 %copy.15 = f32[1,1,2,64]{3,2,1,0:T(2,128)} copy(f32[1,1,2,64]{3,2,1,0:T(2,128)S(1)} %get-tuple-element.2) | data formatting | bytes 1024
  54.2 0.6 %copy.16 = f32[1,1,2,192]{3,2,1,0:T(2,128)} copy(f32[1,1,2,192]{3,2,1,0:T(2,128)S(1)} %get-tuple-element.3) | data formatting | bytes 3072

commit v6 on v5

--- a/solution.py
+++ b/solution.py
@@ -565,6 +565,17 @@
     settle(force_recv, send_a.at[1])
 
 
+def copy_out(energy_in, force_in, energy_out, force_out, sem):
+    copies = [
+        pltpu.make_async_copy(energy_in, energy_out, sem.at[0]),
+        pltpu.make_async_copy(force_in, force_out, sem.at[1]),
+    ]
+    for copy in copies:
+        copy.start()
+    for copy in copies:
+        copy.wait()
+
+
 def on_device(
     positions,
     species,
@@ -640,7 +651,16 @@
         ],
         compiler_params=pltpu.CompilerParams(collective_id=0, has_side_effects=True),
     )(*args)
-    return energies, forces
+    return pl.pallas_call(
+        copy_out,
+        out_shape=(jax.ShapeDtypeStruct((*cells, SLOTS), F32), jax.ShapeDtypeStruct((*cells, 3 * SLOTS), F32)),
+        in_specs=[pl.BlockSpec(memory_space=pl.ANY)] * 2,
+        out_specs=[pl.BlockSpec(memory_space=pl.ANY)] * 2,
+        scratch_shapes=[dma((2,))],
+    )(
+        pltpu.with_memory_space_constraint(energies, pltpu.VMEM),
+        pltpu.with_memory_space_constraint(forces, pltpu.VMEM),
+    )
 
 
 def solution(mesh):

time: 55 us -> 54.4 us (0.989)
  local copies, waits for them, and re-layouts: 1.14 us -> 0 us
  Pallas kernels: 53 us -> 53.6 us
    unnamed x2 -> x0, local copies, waits for them, and re-layouts: 1.14 us -> none
    pallas_call x0 -> x1, Pallas kernels: none -> 0.6 us  [on_device(): pl.pallas_call(copy_out, out_shape=(jax.ShapeDtypeStruct((*cells, SLOTS),...]
where the time goes in v6:
time: 54.4 us; the launch traced here: 54.3 us
  Pallas kernels  53.6 us (99%)
  between operations  0.64 us (1%)
    pallas_call x1, Pallas kernels, on_device(): pl.pallas_call(kernel, out_shape=(pltpu.VMEM((*cells, SLOTS), F32), pltpu...  53 us

profile of v6, /device:TPU:1, one launch (start us, length us, event | category | flops | bytes accessed | tf_op | source)
XLA Modules:
  0.0 54.3 jit_solution(17107797093643720230)
XLA Ops:
  0.6 53.0 %shard_map.122 = (f32[1,1,2,64]{3,2,1,0:T(2,128)S(1)}, f32[1,1,2,192]{3,2,1,0:T(2,128)S(1)}) custom-call(f32[1,1,2,192]{3,2,1,0:T(2,128)} %pos_in.1, s32[1,1,2,64]{3,2,1,0:T(2,128)} %spec_in.1, s32[1,1,2,512]{3,2,1,0:T(2,128)} %nbr_in.1, bf16[5,128]{1,0:T(8,128)(2,1)} %center_in.1, bf16[5,128]{1,0:T(8,128)(2,1)} %neighbor_in.1, bf16[8,128]{1,0:T(8,128)(2,1)} %radial_in.1, ...), custom_call_target="tpu_custom_call" | custom-call | tf_op jit(solution)/shard_map/pallas_call | solution.py:608
  53.7 0.6 %shard_map.123 = (f32[1,1,2,64]{3,2,1,0:T(2,128)}, f32[1,1,2,192]{3,2,1,0:T(2,128)}) custom-call(f32[1,1,2,64]{3,2,1,0:T(2,128)S(1)} %get-tuple-element.4.energy_in, f32[1,1,2,192]{3,2,1,0:T(2,128)S(1)} %get-tuple-element.5.force_in), custom_call_target="tpu_custom_call" | custom-call | tf_op jit(solution)/shard_map/pallas_call | solution.py:654

commit v7 on v6

--- a/solution.py
+++ b/solution.py
@@ -369,10 +369,9 @@
         edge = summed * gate
         upd_d[block, :] = gate + edge * (1.0 - gate)
         edge_buf[block, :] = edge
-        high, low = split_bf16(edge)
         mine = members[0:SLOTS, 0:half_edges]
         own_rows = pl.ds(SLOTS * z, SLOTS)
-        table[4, SLOTS * z : SLOTS * (z + 1), :] = ((dot(mine, high) + dot(mine, low)) * (1.0 / NEIGH)).astype(BF16)
+        table[4, SLOTS * z : SLOTS * (z + 1), :] = (dot(mine, edge.astype(BF16)) * (1.0 / NEIGH)).astype(BF16)
         for k, (dy, dz) in enumerate(PARTNERS):
             if dz == (-1 if z == 0 else 1):
                 continue
@@ -500,13 +499,13 @@
         value_g = gathered(values, j)
         latent_buf[span, :] = dot(diag_at[j], value_g)
         all_g = dot(
-            jnp.concatenate([gathered(mixes, j), value_g], axis=1),
+            jnp.concatenate([gathered(mixes, j)[GROUP:], value_g[GROUP:]], axis=1),
             jnp.concatenate([summed_b[span, :], env_buf[span, :]], axis=1),
             NT,
         )
         for m in range(1, 9):
             angular_g[m].append(
-                jnp.sum(all_g[GROUP * m : GROUP * (m + 1)] * group_mask, axis=0, keepdims=True)
+                jnp.sum(all_g[GROUP * (m - 1) : GROUP * m] * group_mask, axis=0, keepdims=True)
             )
     latent_g = dot(latent_buf[...].astype(BF16), env_ref[...], NT).astype(BF16).astype(F32)
     mixed_g = ((edge_buf[...] + latent_g) * mix_d[...]).astype(BF16)

time: 54.4 us -> 54.3 us (level)
  no operation moved by 1% of the time
where the time goes in v7:
time: 54.3 us; the launch traced here: 54.2 us
  Pallas kernels  53.5 us (99%)
  between operations  0.64 us (1%)
    pallas_call x1, Pallas kernels, on_device(): pl.pallas_call(kernel, out_shape=(pltpu.VMEM((*cells, SLOTS), F32), pltpu...  52.9 us

profile of v7, /device:TPU:1, one launch (start us, length us, event | category | flops | bytes accessed | tf_op | source)
XLA Modules:
  0.0 54.2 jit_solution(23342052838571168)
XLA Ops:
  0.6 52.9 %shard_map.122 = (f32[1,1,2,64]{3,2,1,0:T(2,128)S(1)}, f32[1,1,2,192]{3,2,1,0:T(2,128)S(1)}) custom-call(f32[1,1,2,192]{3,2,1,0:T(2,128)} %pos_in.1, s32[1,1,2,64]{3,2,1,0:T(2,128)} %spec_in.1, s32[1,1,2,512]{3,2,1,0:T(2,128)} %nbr_in.1, bf16[5,128]{1,0:T(8,128)(2,1)} %center_in.1, bf16[5,128]{1,0:T(8,128)(2,1)} %neighbor_in.1, bf16[8,128]{1,0:T(8,128)(2,1)} %radial_in.1, ...), custom_call_target="tpu_custom_call" | custom-call | tf_op jit(solution)/shard_map/pallas_call | solution.py:607
  53.6 0.6 %shard_map.123 = (f32[1,1,2,64]{3,2,1,0:T(2,128)}, f32[1,1,2,192]{3,2,1,0:T(2,128)}) custom-call(f32[1,1,2,64]{3,2,1,0:T(2,128)S(1)} %get-tuple-element.4.energy_in, f32[1,1,2,192]{3,2,1,0:T(2,128)S(1)} %get-tuple-element.5.force_in), custom_call_target="tpu_custom_call" | custom-call | tf_op jit(solution)/shard_map/pallas_call | solution.py:653
